TPU v7x, 512 devices: a whole 4x4x16 slice. The times are simulated.
512 devices in a mesh: seq: 16 (over z), exp: 32 (over y, x, core).
Axes of the slice: x: 4, y: 4, z: 16, core: 2. Of those that a mesh axis runs over, the one named last changes fastest.
Arguments:
- byte_embed: bfloat16 [32, 2048, 1024], P('exp', 'seq'), may hold values from -16 to 16
- score_weight: float32 [1024], replicated, may hold values from -1 to 1
- norm_gain: float32 [1024], replicated, may hold values from 0.25 to 1.75
- router: bfloat16 [1024, 32], replicated, may hold values from -0.1875 to 0.1875
- routes: int32 [32, 512, 2], P('exp', 'seq'), may hold values from 0 to 31, all different within a row; in each aligned block of 32 rows (0 to 31, 32 to 63, ..., all dimensions but the last counted through in order) at most 3 rows name the same one
- expert_in: bfloat16 [32, 1024, 4096], P('exp', None, 'seq'), may hold values from -0.1875 to 0.1875
- expert_out: bfloat16 [32, 4096, 1024], P('exp', 'seq'), may hold values from -0.09375 to 0.09375
- cotangent: bfloat16 [32, 512, 1024], P('exp', 'seq'), may hold values from -6 to 6
Outputs:
- grad_embed: bfloat16 [32, 2048, 1024], P('exp', 'seq')
- grad_in: float32 [32, 1024, 4096], P('exp', None, 'seq')
- grad_out: float32 [32, 4096, 1024], P('exp', 'seq')
Inputs may be any that keep to these rules, and one draw needn't show every extreme that they name: `routes`: among the 32 tokens of one device, at most 3 pairs name the same expert, and some device reaches 3 for some expert. The two experts of a token differ.
All inputs are finite; a program needn't handle non-finite values.
Results may differ from a plain program's by a relative error of at most 0.014.
Values may be sent and summed in bfloat16 or wider, within the bound.
A program may use at most 64 MiB of HBM per device.

v0:
```python
import jax
import jax.numpy as jnp
from jax import lax
from jax.sharding import PartitionSpec as P

SQRT_HALF = 0.7071067811865476
INV_ROOT_TWO_PI = 0.3989422804014327


def front(inputs, norm_gain, score_weight, router, routes):
    batches, length, features = inputs.shape
    highest = lax.Precision.HIGHEST
    quartets = inputs.reshape(batches, length // 4, 4, features)
    pair_means = quartets.reshape(batches, length // 4, 2, 2, features).mean(axis=3)
    quad_mean = quartets.mean(axis=2)
    score_one = jnp.einsum("btqd,d->btq", quartets, score_weight, precision=highest)
    score_two = jnp.repeat(
        jnp.einsum("btpd,d->btp", pair_means, score_weight, precision=highest), 2, axis=2
    )
    score_four = jnp.broadcast_to(
        jnp.einsum("btd,d->bt", quad_mean, score_weight, precision=highest)[:, :, None],
        score_one.shape,
    )
    largest = jnp.maximum(jnp.maximum(score_one, score_two), score_four)
    weight_one = jnp.exp(score_one - largest)
    weight_two = jnp.exp(score_two - largest)
    weight_four = jnp.exp(score_four - largest)
    denominator = weight_one + weight_two + weight_four
    pair_full = jnp.repeat(pair_means, 2, axis=2)
    blended = (
        weight_one[..., None] * quartets
        + weight_two[..., None] * pair_full
        + weight_four[..., None] * quad_mean[:, :, None, :]
    ) / denominator[..., None]
    tokens = blended.mean(axis=2)
    mean_square = jnp.mean(tokens * tokens, axis=-1, keepdims=True)
    normed = tokens * lax.rsqrt(mean_square + 1e-06) * norm_gain
    logits = jnp.einsum("btd,de->bte", normed, router.astype(jnp.float32), precision=highest)
    experts = logits.shape[-1]
    sigmoid_all = 1.0 / (1.0 + jnp.exp(-logits))
    chosen = (routes[..., None] == jnp.arange(experts, dtype=jnp.int32)).astype(jnp.float32)
    picked = jnp.sum(chosen * sigmoid_all[:, :, None, :], axis=-1)
    gate_values = picked / jnp.sum(picked, axis=-1, keepdims=True)
    return (tokens, normed, gate_values)


def deliver(row_stack, gates_in):
    owned_rows, owned_gates = (
        lax.all_to_all(row_stack, "exp", split_axis=1, concat_axis=1, tiled=True),
        lax.all_to_all(gates_in, "exp", split_axis=1, concat_axis=1, tiled=True),
    )
    return (
        lax.all_gather(owned_rows, "seq", axis=1, tiled=True),
        lax.all_gather(owned_gates, "seq", axis=1, tiled=True),
    )


def per_device(
    byte_embed, score_weight, norm_gain, router, routes, expert_in, expert_out, cotangent
):
    experts_all = router.shape[1]
    token_count = routes.shape[1]
    width_model = byte_embed.shape[2]
    capacity = max(2, 3 * token_count // experts_all)
    owners = lax.axis_size("exp")
    slot_count = lax.axis_size("seq") * owners * capacity
    highest = lax.Precision.HIGHEST
    contract_rows = (((0,), (0,)), ((), ()))
    contract_cols = (((1,), (1,)), ((), ()))

    def local_front(values):
        return front(values, norm_gain, score_weight, router, routes)

    (tokens, normed, gate_values), pullback = jax.vjp(local_front, byte_embed.astype(jnp.float32))
    normed_rows = normed[0].astype(jnp.bfloat16)
    route_rows = routes[0]
    onehot = (route_rows[:, :, None] == jnp.arange(experts_all, dtype=jnp.int32)).astype(jnp.int32)
    running = jnp.cumsum(onehot.reshape(2 * token_count, experts_all), axis=0)
    running = running.reshape(token_count, 2, experts_all)
    position = jnp.sum(onehot * (running - 1), axis=2)
    slot_index = route_rows * capacity + position
    matches = (
        slot_index[:, :, None] == jnp.arange(experts_all * capacity, dtype=jnp.int32)
    ).astype(jnp.float32)
    picker = jnp.sum(matches, axis=1).astype(jnp.bfloat16)
    token_buffer = lax.dot_general(
        picker, normed_rows, contract_rows, preferred_element_type=jnp.float32
    )
    cot_buffer = lax.dot_general(
        picker, cotangent[0], contract_rows, preferred_element_type=jnp.float32
    )
    row_buffer = (
        jnp.stack([token_buffer, cot_buffer])
        .astype(jnp.bfloat16)
        .reshape(2, experts_all, capacity, width_model)
    )
    gate_buffer = jnp.einsum("tks,tk->s", matches, gate_values[0], precision=highest)
    gate_buffer = gate_buffer.astype(jnp.bfloat16).reshape(1, experts_all, capacity)
    weight_in = expert_in[0]
    weight_out = expert_out[0]
    both_rows, slot_gates = deliver(row_buffer, gate_buffer)
    token_rows = both_rows[0].reshape(slot_count, width_model)
    cot_rows = both_rows[1].reshape(slot_count, width_model)
    gate_first = slot_gates.reshape(slot_count).astype(jnp.float32)
    preact = jnp.dot(token_rows, weight_in, preferred_element_type=jnp.float32)
    normal_cdf = 0.5 * (1.0 + jax.scipy.special.erf(preact * SQRT_HALF))
    normal_pdf = INV_ROOT_TWO_PI * jnp.exp(-0.5 * preact * preact)
    hidden = preact * normal_cdf
    upstream = lax.dot_general(
        cot_rows, weight_out, contract_cols, preferred_element_type=jnp.float32
    )
    gate_terms = jnp.sum(hidden * upstream, axis=1)
    hidden_grad = (gate_first[:, None] * upstream * (normal_cdf + preact * normal_pdf)).astype(
        jnp.bfloat16
    )
    gated_hidden = (gate_first[:, None] * hidden).astype(jnp.bfloat16)
    grad_out = lax.dot_general(
        gated_hidden, cot_rows, contract_rows, preferred_element_type=jnp.float32
    )
    grad_in = lax.dot_general(
        token_rows, hidden_grad, contract_rows, preferred_element_type=jnp.float32
    )
    own_slots = owners * capacity
    summed_rows = lax.psum_scatter(
        lax.dot_general(
            hidden_grad, weight_in, contract_cols, preferred_element_type=jnp.float32
        ).astype(jnp.bfloat16),
        "seq",
        scatter_dimension=0,
        tiled=True,
    )
    every_term = lax.psum(gate_terms, "seq")
    own_terms = lax.dynamic_slice_in_dim(
        every_term, lax.axis_index("seq") * own_slots, own_slots, 0
    )
    returned_rows, returned_gates = (
        lax.all_to_all(
            summed_rows.reshape(owners, capacity, width_model),
            "exp",
            split_axis=0,
            concat_axis=0,
            tiled=True,
        ),
        lax.all_to_all(
            own_terms.astype(jnp.bfloat16).reshape(owners, capacity),
            "exp",
            split_axis=0,
            concat_axis=0,
            tiled=True,
        ),
    )
    normed_grad = jnp.dot(
        picker,
        returned_rows.reshape(experts_all * capacity, width_model),
        preferred_element_type=jnp.float32,
    )
    gate_grad = jnp.einsum(
        "tks,s->tk", matches, returned_gates.reshape(-1).astype(jnp.float32), precision=highest
    )
    (embed_grad,) = pullback((cotangent.astype(jnp.float32), normed_grad[None], gate_grad[None]))
    return (embed_grad.astype(jnp.bfloat16), grad_in[None], grad_out[None])


def solution(mesh):
    in_specs = (
        P("exp", "seq", None),
        P(),
        P(),
        P(),
        P("exp", "seq", None),
        P("exp", None, "seq"),
        P("exp", "seq", None),
        P("exp", "seq", None),
    )
    out_specs = (P("exp", "seq", None), P("exp", None, "seq"), P("exp", "seq", None))
    return jax.shard_map(
        per_device, mesh=mesh, in_specs=in_specs, out_specs=out_specs, check_vma=False
    )
```

profile of v0, /device:TPU:1, one launch (start us, length us, event | category | flops | bytes accessed | tf_op | source)
XLA Modules:
  0.0 291.5 jit_solution(9137847497761137692)
XLA Ops:
  7.2 1.4 reshape.708
  8.6 1.1 reshape.709
  13.9 1.1 fusion.21
  18.0 20.4 %all_to_all.25 = bf16[2,32,3,1024]{3,0,2,1:T(2,128)(2,1)} all-to-all(bf16[2,32,3,1024]{3,0,2,1:T(2,128)(2,1)S(1)} %copy.132), channel_id=1, replica_groups=mesh['seq'=16,'exp'=32] {'exp'}, dimensions={1} | all-to-all | bytes 786432 | tf_op jit(solution)/shard_map/all_to_all | solution.py:49
  38.5 0.9 add_divide_fusion.1
  40.2 10.5 %all_to_all.26 = bf16[1,32,3]{2,0,1:T(2,128)(2,1)S(1)} all-to-all(bf16[1,32,3]{2,0,1:T(2,128)(2,1)S(1)} %reshape.729), channel_id=1, replica_groups=mesh['seq'=16,'exp'=32] {'exp'}, dimensions={1} | all-to-all | bytes 384 | tf_op jit(solution)/shard_map/all_to_all | solution.py:50
  50.7 33.3 %all_gather.6 = bf16[1,512,3]{2,0,1:T(2,128)(2,1)S(1)} all-gather(bf16[1,32,3]{2,0,1:T(2,128)(2,1)S(1)} %all_to_all.26), channel_id=1, replica_groups=mesh['seq'=16,'exp'=32] {'seq'}, dimensions={1}, use_global_device_ids=true | all-gather | bytes 3264 | tf_op jit(solution)/shard_map/all_gather | solution.py:54
  85.0 38.5 %all-gather.2.cloned.1.call-done = bf16[2,512,3,1024]{3,0,2,1:T(2,128)(2,1)} async-done(((bf16[2,32,3,1024]{3,0,2,1:T(2,128)(2,1)}), bf16[2,512,3,1024]{3,0,2,1:T(2,128)(2,1)}) %all-gather.2.cloned.1.call-update) | async-done | bytes 6291472 | tf_op jit(solution)/shard_map/all_gather | solution.py:53
  123.6 34.7 %slice_reduce_fusion = (bf16[512,3,1024]{2,1,0:T(4,128)(2,1)}, bf16[512,3,1024]{2,1,0:T(4,128)(2,1)}) fusion(bf16[2,512,3,1024]{3,0,2,1:T(2,128)(2,1)} %all-gather.2.cloned.1.call-done), kind=kLoop, calls=%fused_computation | loop fusion | bytes 12582912 | tf_op jit(solution)/shard_map/slice | solution.py:102
  158.3 8.8 %reshape_squeeze.6 = bf16[1536,1024]{1,0:T(8,128)(2,1)} reshape(bf16[512,3,1024]{2,1,0:T(4,128)(2,1)} %get-tuple-element.4) | data formatting | bytes 6291456 | tf_op jit(solution)/shard_map/reshape;squeeze | solution.py:103
  167.1 8.9 %reshape_squeeze.7 = bf16[1536,1024]{1,0:T(8,128)(2,1)} reshape(bf16[512,3,1024]{2,1,0:T(4,128)(2,1)} %get-tuple-element.3) | data formatting | bytes 6291456 | tf_op jit(solution)/shard_map/reshape;squeeze | solution.py:102
  176.0 3.0 %fusion.18 = f32[1536,256]{0,1:T(8,128)S(1)} fusion(bf16[1536,1024]{1,0:T(8,128)(2,1)} %reshape_squeeze.6, bf16[1,256,1024]{2,1,0:T(8,128)(2,1)S(1)} %copy-done.50), kind=kOutput, calls=%fused_computation.34 | convolution fusion | flops 805306368 | bytes 5242880 | tf_op jit(solution)/shard_map/dot_general | solution.py:109
  179.1 3.4 %fusion.5 = (bf16[1536,256]{0,1:T(8,128)(2,1)S(1)}, f32[1536]{0:T(1024)}, f32[1536,256]{0,1:T(8,128)}) fusion(f32[1536,256]{0,1:T(8,128)S(1)} %fusion.18, f32[1536]{0:T(1024)S(1)} %reshape.717, bf16[1536,1024]{1,0:T(8,128)(2,1)S(1)} %copy-done.2, bf16[1,1024,256]{2,1,0:T(8,128)(2,1)S(1)} %copy-done), kind=kOutput, calls=%fused_computation.9 | convolution fusion | flops 810809856 | bytes 7614464 | tf_op jit(solution)/shard_map/dot_general | solution.py:105
  182.5 2.7 convolution_convert_fusion
  189.5 0.8 copy.135
  190.8 1.0 mul.511
  192.1 24.7 %psum.7 = bf16[1536]{0:T(1024)(128)(2,1)S(1)} all-reduce(f32[1536]{0:T(1024)S(1)} %copy-done.34), channel_id=1, replica_groups=mesh['seq'=16,'exp'=32] {'seq'}, use_global_device_ids=true, to_apply=%region_11.12 | all-reduce | flops 1536 | bytes 9216 | tf_op jit(solution)/shard_map/psum | solution.py:132
  217.6 14.2 %all-to-all-start.3 = ((bf16[32,1,3]{2,1,0:T(2,128)(2,1)}), bf16[32,1,3]{2,1,0:T(2,128)(2,1)S(1)}, u32[]{:S(2)}, u32[]{:S(2)}) async-start(bf16[32,1,3]{2,1,0:T(2,128)(2,1)} %all_to_all.20), calls=%async_computation.4 | async-start | bytes 32768 | tf_op jit(solution)/shard_map/all_to_all | solution.py:144
  231.8 4.5 %convolution_bitcast_fusion = f32[1,256,1024]{2,1,0:T(8,128)} fusion(bf16[1536,1024]{1,0:T(8,128)(2,1)} %reshape_squeeze.6, f32[1536]{0:T(1024)S(1)} %copy-done.33, f32[1536,256]{0,1:T(8,128)} %get-tuple-element.27), kind=kOutput, calls=%fused_computation.13 | convolution fusion | flops 807665664 | bytes 5773312 | tf_op jit(solution)/shard_map/dot_general | solution.py:117
  236.4 2.0 convolution_bitcast_fusion.1
  239.3 12.9 %reduce-scatter.2.cloned.1.call-done = bf16[96,1024]{1,0:T(8,128)(2,1)} async-done(((bf16[1536,1024]{1,0:T(8,128)(2,1)}), bf16[96,1024]{1,0:T(8,128)(2,1)}) %reduce-scatter.2.cloned.1.call-update) | async-done | bytes 196624 | tf_op jit(solution)/shard_map/reduce_scatter | solution.py:124
  252.2 1.7 reshape.713
  253.9 16.5 %all-to-all-start.2 = ((bf16[32,3,1024]{2,1,0:T(4,128)(2,1)}), bf16[32,3,1024]{2,1,0:T(4,128)(2,1)S(1)}, u32[]{:S(2)}, u32[]{:S(2)}) async-start(bf16[32,3,1024]{2,1,0:T(4,128)(2,1)} %reshape.713), calls=%async_computation.3 | async-start | bytes 524288 | tf_op jit(solution)/shard_map/all_to_all | solution.py:137
  270.7 8.6 %all-to-all-done.2 = bf16[32,3,1024]{2,1,0:T(4,128)(2,1)S(1)} async-done(((bf16[32,3,1024]{2,1,0:T(4,128)(2,1)}), bf16[32,3,1024]{2,1,0:T(4,128)(2,1)S(1)}, u32[]{:S(2)}, u32[]{:S(2)}) %all-to-all-start.2) | async-done | bytes 196640 | tf_op jit(solution)/shard_map/all_to_all | solution.py:137
  (190 shorter events, 20.8 us)
Async XLA Ops:
  7.2 171.9 %copy-start = (bf16[1,1024,256]{2,1,0:T(8,128)(2,1)S(1)}, bf16[1,1024,256]{2,1,0:T(8,128)(2,1)}, u32[]{:S(2)}) copy-start(bf16[1,1024,256]{2,1,0:T(8,128)(2,1)} %param.13) | copy-start | bytes 1572868
  7.2 116.4 %all-gather.2.cloned.1.call-start = ((), (), s32[]{:S(2)}) async-start(), calls=%async_computation.5 | async-start | bytes 6684672 | tf_op jit(solution)/shard_map/all_gather | solution.py:53
  13.9 172.0 %copy-start.7 = (f32[32,4]{1,0:T(8,128)}, f32[32,4]{1,0:T(8,128)S(1)}, u32[]{:S(2)}) copy-start(f32[32,4]{1,0:T(8,128)S(1)} %get-tuple-element.20) | copy-start | bytes 1540
  13.9 173.2 %copy-start.9 = (f32[32,4]{1,0:T(8,128)}, f32[32,4]{1,0:T(8,128)S(1)}, u32[]{:S(2)}) copy-start(f32[32,4]{1,0:T(8,128)S(1)} %get-tuple-element.22) | copy-start | bytes 1540
  16.5 23.0 %copy-start.40 = (s32[32,2]{0,1:T(2,128)}, s32[32,2]{0,1:T(2,128)S(1)}, u32[]{:S(2)}) copy-start(s32[32,2]{0,1:T(2,128)S(1)} %multiply_add_fusion.2) | copy-start | bytes 772
  17.1 21.3 %copy-start.11 = (bf16[1024,32]{0,1:T(8,128)(2,1)S(1)}, bf16[1024,32]{0,1:T(8,128)(2,1)}, u32[]{:S(2)}) copy-start(bf16[1024,32]{0,1:T(8,128)(2,1)} %param.11) | copy-start | bytes 196612
  38.4 213.8 %reduce-scatter.2.cloned.1.call-start = ((), (), s32[]{:S(2)}) async-start(), calls=%async_computation.6 | async-start | bytes 3342336 | tf_op jit(solution)/shard_map/reduce_scatter | solution.py:124
  39.5 118.8 %copy-start.28 = (f32[32,2]{0,1:T(2,128)}, f32[32,2]{0,1:T(2,128)S(1)}, u32[]{:S(2)}) copy-start(f32[32,2]{0,1:T(2,128)S(1)} %get-tuple-element.12) | copy-start | bytes 772
  85.0 94.0 %copy-start.32 = (f32[1536]{0:T(1024)}, f32[1536]{0:T(1024)S(1)}, u32[]{:S(2)}) copy-start(f32[1536]{0:T(1024)S(1)} %reshape.717) | copy-start | bytes 18436
  167.1 8.9 %copy-start.50 = (bf16[1,256,1024]{2,1,0:T(8,128)(2,1)S(1)}, bf16[1,256,1024]{2,1,0:T(8,128)(2,1)}, u32[]{:S(2)}) copy-start(bf16[1,256,1024]{2,1,0:T(8,128)(2,1)} %param.14) | copy-start | bytes 1572868
  188.2 3.9 %copy-start.34 = (f32[1536]{0:T(1024)S(1)}, f32[1536]{0:T(1024)}, u32[]{:S(2)}) copy-start(f32[1536]{0:T(1024)} %get-tuple-element.16) | copy-start | bytes 18436
  188.2 43.6 %copy-start.33 = (f32[1536]{0:T(1024)S(1)}, f32[1536]{0:T(1024)}, u32[]{:S(2)}) copy-start(f32[1536]{0:T(1024)} %copy-done.32) | copy-start | bytes 18436
  217.6 21.1 %all-to-all-start.3 = ((bf16[32,1,3]{2,1,0:T(2,128)(2,1)}), bf16[32,1,3]{2,1,0:T(2,128)(2,1)S(1)}, u32[]{:S(2)}, u32[]{:S(2)}) async-start(bf16[32,1,3]{2,1,0:T(2,128)(2,1)} %all_to_all.20), calls=%async_computation.4 | async-start | bytes 32768 | tf_op jit(solution)/shard_map/all_to_all | solution.py:144
  231.8 4.5 %copy-start.3 = (bf16[1536,1024]{1,0:T(8,128)(2,1)S(1)}, bf16[1536,1024]{1,0:T(8,128)(2,1)}, u32[]{:S(2)}) copy-start(bf16[1536,1024]{1,0:T(8,128)(2,1)} %reshape_squeeze.7) | copy-start | bytes 9437188
  236.3 34.1 %copy-start.12 = (bf16[1024,32]{0,1:T(8,128)(2,1)S(1)}, bf16[1024,32]{0,1:T(8,128)(2,1)}, u32[]{:S(2)}) copy-start(bf16[1024,32]{0,1:T(8,128)(2,1)} %param.11) | copy-start | bytes 196612
  236.3 34.1 %copy-start.23 = (f32[32,32]{1,0:T(8,128)S(1)}, f32[32,32]{1,0:T(8,128)}, u32[]{:S(2)}) copy-start(f32[32,32]{1,0:T(8,128)} %get-tuple-element.26) | copy-start | bytes 12292
  238.4 41.1 %copy-start.20 = (bf16[32,96]{1,0:T(8,128)(2,1)S(1)}, bf16[32,96]{1,0:T(8,128)(2,1)}, u32[]{:S(2)}) copy-start(bf16[32,96]{1,0:T(8,128)(2,1)} %copy-done.19) | copy-start | bytes 18436
  238.4 41.1 %copy-start.25 = (f32[1024]{0:T(1024)S(1)}, f32[1024]{0:T(1024)}, u32[]{:S(2)}) copy-start(f32[1024]{0:T(1024)} %param.10) | copy-start | bytes 12292
  238.4 41.5 %copy-start.49 = (f32[32]{0:T(128)S(1)}, f32[32]{0:T(128)}, u32[]{:S(2)}) copy-start(f32[32]{0:T(128)} %copy-done.48) | copy-start | bytes 388
  238.4 41.5 %copy-start.14 = (bf16[1,32,1024]{2,1,0:T(8,128)(2,1)S(1)}, bf16[1,32,1024]{2,1,0:T(8,128)(2,1)}, u32[]{:S(2)}) copy-start(bf16[1,32,1024]{2,1,0:T(8,128)(2,1)} %param.15) | copy-start | bytes 196612
  238.4 41.5 %copy-start.47 = (f32[32]{0:T(128)S(1)}, f32[32]{0:T(128)}, u32[]{:S(2)}) copy-start(f32[32]{0:T(128)} %get-tuple-element.23) | copy-start | bytes 388
  238.4 41.6 %copy-start.5 = (f32[32,1024]{1,0:T(8,128)S(1)}, f32[32,1024]{1,0:T(8,128)}, u32[]{:S(2)}) copy-start(f32[32,1024]{1,0:T(8,128)} %copy-done.4) | copy-start | bytes 393220
  238.4 41.6 %copy-start.10 = (f32[32,4]{1,0:T(8,128)S(1)}, f32[32,4]{1,0:T(8,128)}, u32[]{:S(2)}) copy-start(f32[32,4]{1,0:T(8,128)} %copy-done.9) | copy-start | bytes 1540
  253.9 25.4 %all-to-all-start.2 = ((bf16[32,3,1024]{2,1,0:T(4,128)(2,1)}), bf16[32,3,1024]{2,1,0:T(4,128)(2,1)S(1)}, u32[]{:S(2)}, u32[]{:S(2)}) async-start(bf16[32,3,1024]{2,1,0:T(4,128)(2,1)} %reshape.713), calls=%async_computation.3 | async-start | bytes 524288 | tf_op jit(solution)/shard_map/all_to_all | solution.py:137
  (31 other events, 62.2 us)
Sparse Core Ops, SparseCore 0:
  38.5 85.0 all-gather.1
  185.3 66.7 reduce-scatter.1
where the time goes:
time: 292 us
  blocking collectives  88.9 us (30%)
  local copies, waits for them, and re-layouts  70.2 us (24%)
  waiting for transfers between devices  60.4 us (21%)
  starting transfers between devices  30.8 us (11%)
  matrix products  19.3 us (7%)
  between operations  15 us (5%)
  other arithmetic  6.98 us (2%)
    all_gather x1, waiting for transfers between devices, deliver(): lax.all_gather(owned_rows, 'seq', axis=1, tiled=True)  38.5 us
    slice x1, local copies, waits for them, and re-layouts, per_device(): token_rows = both_rows[0].reshape(slot_count, width_model)  34.7 us
    all_gather x1, blocking collectives, deliver(): lax.all_gather(owned_gates, 'seq', axis=1, tiled=True)  33.3 us
    psum x1, blocking collectives, per_device(): every_term = lax.psum(gate_terms, 'seq')  24.7 us
    all_to_all x1, blocking collectives, deliver(): lax.all_to_all(row_stack, 'exp', split_axis=1, concat_axis=1, tiled=True)  20.4 us
    all_to_all x1, starting transfers between devices, per_device(): lax.all_to_all(summed_rows.reshape(owners, capacity, width_model), 'exp',...  16.5 us
    all_to_all x1, starting transfers between devices, per_device(): lax.all_to_all(own_terms.astype(jnp.bfloat16).reshape(owners, capacity),...  14.2 us
    reduce_scatter x1, waiting for transfers between devices, per_device(): lax.psum_scatter(lax.dot_general(hidden_grad, weight_in, contract_cols, p...  12.9 us
  transfers between devices with their start and end apart: 4, of which 4 were waited for; matrix products, arithmetic and copies ran while one was open for 6% of the time, Pallas kernels for 0%

commit v1 on v0

v1 whole, which is shorter than its diff:
```python
import functools

import jax
import jax.numpy as jnp
from jax import lax
from jax.experimental import pallas as pl
from jax.experimental.pallas import tpu as pltpu
from jax.sharding import PartitionSpec as P

SQRT_HALF = 0.7071067811865476
INV_ROOT_TWO_PI = 0.3989422804014327
MESH = pl.DeviceIdType.MESH
LANES = 128
SPLIT = 48
ROWS = (((0,), (0,)), ((), ()))
COLS = (((1,), (1,)), ((), ()))
F32 = jnp.float32
BF16 = jnp.bfloat16


def front(inputs, norm_gain, score_weight, router, routes):
    batches, length, features = inputs.shape
    highest = lax.Precision.HIGHEST
    quartets = inputs.reshape(batches, length // 4, 4, features)
    pair_means = quartets.reshape(batches, length // 4, 2, 2, features).mean(axis=3)
    quad_mean = quartets.mean(axis=2)
    score_one = jnp.einsum("btqd,d->btq", quartets, score_weight, precision=highest)
    score_two = jnp.repeat(
        jnp.einsum("btpd,d->btp", pair_means, score_weight, precision=highest), 2, axis=2
    )
    score_four = jnp.broadcast_to(
        jnp.einsum("btd,d->bt", quad_mean, score_weight, precision=highest)[:, :, None],
        score_one.shape,
    )
    largest = jnp.maximum(jnp.maximum(score_one, score_two), score_four)
    weight_one = jnp.exp(score_one - largest)
    weight_two = jnp.exp(score_two - largest)
    weight_four = jnp.exp(score_four - largest)
    denominator = weight_one + weight_two + weight_four
    pair_full = jnp.repeat(pair_means, 2, axis=2)
    blended = (
        weight_one[..., None] * quartets
        + weight_two[..., None] * pair_full
        + weight_four[..., None] * quad_mean[:, :, None, :]
    ) / denominator[..., None]
    tokens = blended.mean(axis=2)
    mean_square = jnp.mean(tokens * tokens, axis=-1, keepdims=True)
    normed = tokens * lax.rsqrt(mean_square + 1e-06) * norm_gain
    logits = jnp.einsum("btd,de->bte", normed, router.astype(F32), precision=highest)
    experts = logits.shape[-1]
    chosen = (routes[..., None] == jnp.arange(experts, dtype=jnp.int32)).astype(F32)
    picked = jnp.sum(chosen * logits[:, :, None, :], axis=-1)
    return (tokens, normed, picked)


def expert_ring(
    steps,
    slots,
    x_ref,
    c_ref,
    win_ref,
    wout_ref,
    gin_ref,
    gout_ref,
    rows_ref,
    gate_ref,
    xs,
    cs,
    hid,
    hgrad,
    part,
    gpart,
    take,
    give,
    gtake,
    ggive,
    ag_send,
    ag_recv,
    rs_send,
    rs_recv,
    rg_send,
    rg_recv,
):
    me = lax.axis_index("seq")
    half = steps // 2
    right = lax.rem(me + 1, steps)
    left = lax.rem(me + steps - 1, steps)
    width = x_ref.shape[1]
    block = width // half

    def rows_of(index, start=0, size=slots):
        return pl.ds(pl.multiple_of(index * slots + start, 16), size)

    def source(way, j):
        return lax.rem(me - j + steps, steps) if way == 0 else lax.rem(me + j, steps)

    def gather(way, j, sub, own=False):
        buf = cs if sub else xs
        place = rows_of(source(way, j))
        src = (c_ref if sub else x_ref) if own else buf.at[place]
        return pltpu.make_async_remote_copy(
            src_ref=src,
            dst_ref=buf.at[place],
            send_sem=ag_send.at[way, j, sub],
            recv_sem=ag_recv.at[way, j, sub],
            device_id={"seq": left if way else right},
            device_id_type=MESH,
        )

    def arrival(way, j, sub):
        buf = cs if sub else xs
        place = rows_of(source(way, j + 1))
        return pltpu.make_async_remote_copy(
            src_ref=buf.at[place],
            dst_ref=buf.at[place],
            send_sem=ag_send.at[way, j, sub],
            recv_sem=ag_recv.at[way, j, sub],
            device_id={"seq": left if way else right},
            device_id_type=MESH,
        )

    def target(way, s):
        return lax.rem(me + half - s, steps) if way == 0 else lax.rem(me + half + s, steps)

    def scatter(way, s, sub, direct=False):
        at = way * half + s
        place = rows_of(at, sub * SPLIT, SPLIT)
        src = part.at[rows_of(target(way, s), sub * SPLIT, SPLIT)] if direct else give.at[place]
        return pltpu.make_async_remote_copy(
            src_ref=src,
            dst_ref=take.at[place],
            send_sem=rs_send.at[way, s, sub],
            recv_sem=rs_recv.at[way, s, sub],
            device_id={"seq": left if way else right},
            device_id_type=MESH,
        )

    def scatter_gate(way, s, direct=False):
        at = way * half + s
        src = gpart.at[target(way, s)] if direct else ggive.at[at]
        return pltpu.make_async_remote_copy(
            src_ref=src,
            dst_ref=gtake.at[at],
            send_sem=rg_send.at[way, s],
            recv_sem=rg_recv.at[way, s],
            device_id={"seq": left if way else right},
            device_id_type=MESH,
        )

    def compute(index):
        place = rows_of(index)
        x = xs[place, :]
        c = cs[place, :]
        pre = jnp.dot(x, win_ref[...], preferred_element_type=F32)
        up = lax.dot_general(c, wout_ref[...], COLS, preferred_element_type=F32)
        cdf = 0.5 * (1.0 + lax.erf(pre * SQRT_HALF))
        pdf = INV_ROOT_TWO_PI * jnp.exp(-0.5 * pre * pre)
        hidden = pre * cdf
        hg = (up * (cdf + pre * pdf)).astype(BF16)
        hid[place, :] = hidden.astype(BF16)
        hgrad[place, :] = hg
        part[place, :] = lax.dot_general(
            hg, win_ref[...], COLS, preferred_element_type=F32
        ).astype(BF16)
        prod = hidden * up
        high = prod.astype(BF16)
        low = (prod - high.astype(F32)).astype(BF16)
        ones = jnp.ones((8, prod.shape[1]), BF16)
        total = lax.dot_general(ones, high, COLS, preferred_element_type=F32)
        total = total + lax.dot_general(ones, low, COLS, preferred_element_type=F32)
        gpart[index, :, 0:slots] = total

    barrier = pltpu.get_barrier_semaphore()
    for peer in (left, right):
        pl.semaphore_signal(barrier, inc=1, device_id={"seq": peer}, device_id_type=MESH)
    pl.semaphore_wait(barrier, 2)

    for sub in range(2):
        for way in range(2):
            gather(way, 0, sub, own=True).start()
    gpart[...] = jnp.zeros_like(gpart)
    xs[rows_of(me), :] = x_ref[...]
    cs[rows_of(me), :] = c_ref[...]
    compute(me)

    def ring_step(j, carry):
        for sub in range(2):
            for way in range(2):
                arrival(way, j - 1, sub).wait_recv()
                gather(way, j, sub).start()
        compute(source(0, j))
        compute(source(1, j))
        return carry

    lax.fori_loop(1, half - 1, ring_step, 0)

    last = half - 1
    for sub in range(2):
        for way in range(2):
            arrival(way, last - 1, sub).wait_recv()
            if sub == way:
                gather(way, last, sub).start()
    compute(source(0, last))
    compute(source(1, last))
    arrival(0, last, 0).wait_recv()
    arrival(1, last, 1).wait_recv()
    compute(source(0, half))

    def weights(s):
        span = pl.ds(pl.multiple_of(s * block, LANES), block)
        gin_ref[span, :] = lax.dot_general(
            xs[:, span], hgrad[...], ROWS, preferred_element_type=F32
        )
        gout_ref[:, span] = lax.dot_general(
            hid[...], cs[:, span], ROWS, preferred_element_type=F32
        )

    def merge(way, s, sub):
        at = way * half + s
        mine = part[rows_of(target(way, s), sub * SPLIT, SPLIT), :].astype(F32)
        came = take[rows_of(at - 1, sub * SPLIT, SPLIT), :].astype(F32)
        give[rows_of(at, sub * SPLIT, SPLIT), :] = (mine + came).astype(BF16)

    scatter(0, 0, 0, direct=True).start()
    scatter(1, 0, 1, direct=True).start()
    scatter_gate(0, 0, direct=True).start()
    scatter(0, 1, 1, direct=True).start()
    scatter(1, 1, 0, direct=True).start()
    scatter_gate(1, 1, direct=True).start()
    weights(0)
    scatter(0, 0, 0, direct=True).wait_recv()
    merge(0, 1, 0)
    scatter(0, 1, 0).start()
    scatter(1, 0, 1, direct=True).wait_recv()
    merge(1, 1, 1)
    scatter(1, 1, 1).start()
    scatter_gate(0, 0, direct=True).wait_recv()
    ggive[1] = gpart[target(0, 1)] + gtake[0]
    scatter_gate(0, 1).start()
    weights(1)

    def scatter_step(s, carry):
        for order in range(2):
            for way in range(2):
                sub = (1 - order) if way == 0 else order
                scatter(way, s - 1, sub).wait_recv()
                merge(way, s, sub)
                scatter(way, s, sub).start()
        for way in range(2):
            scatter_gate(way, s - 1).wait_recv()
            at = way * half + s
            ggive[at] = gpart[target(way, s)] + gtake[at - 1]
            scatter_gate(way, s).start()
        weights(s)
        return carry

    lax.fori_loop(2, half, scatter_step, 0)

    for sub in range(2):
        total = part[rows_of(me, sub * SPLIT, SPLIT), :].astype(F32)
        for way in range(2):
            scatter(way, last, sub).wait_recv()
            total = total + take[rows_of(way * half + last, sub * SPLIT, SPLIT), :].astype(F32)
        rows_ref[pl.ds(sub * SPLIT, SPLIT), :] = total.astype(BF16)
    gate_total = gpart[me]
    for way in range(2):
        scatter_gate(way, last).wait_recv()
        gate_total = gate_total + gtake[way * half + last]
    gate_ref[...] = gate_total

    for way in range(2):
        for sub in range(2):
            gather(way, 0, sub, own=True).wait_send()
    for way in range(2):
        for s in range(half):
            for sub in range(2):
                if s >= 1 and (s < last or sub == way):
                    gather(way, s, sub).wait_send()
                if s >= 1 or sub == way:
                    scatter(way, s, sub).wait_send()
            if s >= 1 or way == 0:
                scatter_gate(way, s).wait_send()


def run_ring(x_rows, c_rows, weight_in, weight_out):
    steps = lax.axis_size("seq")
    slots, width = x_rows.shape
    hidden = weight_in.shape[1]
    half = steps // 2
    vmem = pl.BlockSpec(memory_space=pltpu.VMEM)
    return pl.pallas_call(
        functools.partial(expert_ring, steps, slots),
        out_shape=(
            jax.ShapeDtypeStruct((width, hidden), F32),
            jax.ShapeDtypeStruct((hidden, width), F32),
            jax.ShapeDtypeStruct((slots, width), BF16),
            jax.ShapeDtypeStruct((8, LANES), F32),
        ),
        in_specs=[vmem] * 4,
        out_specs=(vmem,) * 4,
        scratch_shapes=[
            pltpu.VMEM((steps * slots, width), BF16),
            pltpu.VMEM((steps * slots, width), BF16),
            pltpu.VMEM((steps * slots, hidden), BF16),
            pltpu.VMEM((steps * slots, hidden), BF16),
            pltpu.VMEM((steps * slots, width), BF16),
            pltpu.VMEM((steps, 8, LANES), F32),
            pltpu.VMEM((steps * slots, width), BF16),
            pltpu.VMEM((steps * slots, width), BF16),
            pltpu.VMEM((steps, 8, LANES), F32),
            pltpu.VMEM((steps, 8, LANES), F32),
            pltpu.SemaphoreType.DMA((2, half, 2)),
            pltpu.SemaphoreType.DMA((2, half, 2)),
            pltpu.SemaphoreType.DMA((2, half, 2)),
            pltpu.SemaphoreType.DMA((2, half, 2)),
            pltpu.SemaphoreType.DMA((2, half)),
            pltpu.SemaphoreType.DMA((2, half)),
        ],
        compiler_params=pltpu.CompilerParams(
            collective_id=0, has_side_effects=True, vmem_limit_bytes=48 * 1024 * 1024
        ),
    )(x_rows, c_rows, weight_in, weight_out)


def per_device(
    byte_embed, score_weight, norm_gain, router, routes, expert_in, expert_out, cotangent
):
    experts_all = router.shape[1]
    token_count = routes.shape[1]
    width_model = byte_embed.shape[2]
    capacity = max(2, 3 * token_count // experts_all)
    slots = experts_all * capacity
    highest = lax.Precision.HIGHEST

    def local_front(values):
        return front(values, norm_gain, score_weight, router, routes)

    (tokens, normed, picked), pullback = jax.vjp(local_front, byte_embed.astype(F32))
    sigmoids = 1.0 / (1.0 + jnp.exp(-picked[0]))
    gates = sigmoids / jnp.sum(sigmoids, axis=-1, keepdims=True)
    normed_rows = normed[0].astype(BF16)
    route_rows = routes[0]
    onehot = (route_rows[:, :, None] == jnp.arange(experts_all, dtype=jnp.int32)).astype(jnp.int32)
    running = jnp.cumsum(onehot.reshape(2 * token_count, experts_all), axis=0)
    running = running.reshape(token_count, 2, experts_all)
    position = jnp.sum(onehot * (running - 1), axis=2)
    slot_index = route_rows * capacity + position
    matches = (slot_index[:, :, None] == jnp.arange(slots, dtype=jnp.int32)).astype(F32)
    picker = jnp.sum(matches, axis=1).astype(BF16)
    gate_buffer = jnp.sum(jnp.sum(matches * gates[:, :, None], axis=1), axis=0)
    token_buffer = lax.dot_general(picker, normed_rows, ROWS, preferred_element_type=F32)
    cot_buffer = lax.dot_general(picker, cotangent[0], ROWS, preferred_element_type=F32)
    cot_buffer = cot_buffer * gate_buffer[:, None]
    row_buffer = (
        jnp.stack([token_buffer, cot_buffer])
        .astype(BF16)
        .reshape(2, experts_all, capacity, width_model)
    )
    owned = lax.all_to_all(row_buffer, "exp", split_axis=1, concat_axis=1, tiled=True)
    owned = owned.reshape(2, slots, width_model)
    grad_in, grad_out, own_rows, own_terms = run_ring(
        owned[0], owned[1], expert_in[0], expert_out[0]
    )
    extra = jnp.broadcast_to(own_terms[0, :slots].astype(BF16)[:, None], (slots, LANES))
    back = jnp.concatenate([own_rows, extra], axis=1).reshape(experts_all, capacity, -1)
    returned = lax.all_to_all(back, "exp", split_axis=0, concat_axis=0, tiled=True)
    returned = returned.reshape(slots, width_model + LANES)
    normed_grad = jnp.dot(picker, returned[:, :width_model], preferred_element_type=F32)
    scaled = jnp.einsum(
        "tks,s->tk", matches, returned[:, width_model].astype(F32), precision=highest
    )
    picked_grad = (1.0 - sigmoids) * (scaled - gates * jnp.sum(scaled, axis=-1, keepdims=True))
    (embed_grad,) = pullback((cotangent.astype(F32), normed_grad[None], picked_grad[None]))
    return (embed_grad.astype(BF16), grad_in[None], grad_out[None])


def solution(mesh):
    in_specs = (
        P("exp", "seq", None),
        P(),
        P(),
        P(),
        P("exp", "seq", None),
        P("exp", None, "seq"),
        P("exp", "seq", None),
        P("exp", "seq", None),
    )
    out_specs = (P("exp", "seq", None), P("exp", None, "seq"), P("exp", "seq", None))
    return jax.shard_map(
        per_device, mesh=mesh, in_specs=in_specs, out_specs=out_specs, check_vma=False
    )
```

time: 292 us -> 192 us (0.66)
  Pallas kernels: 0 us -> 108 us
  blocking collectives: 88.9 us -> 19.7 us
  waiting for transfers between devices: 60.4 us -> 1.58 us
  local copies, waits for them, and re-layouts: 70.2 us -> 35.7 us
  starting transfers between devices: 30.8 us -> 10.9 us
  matrix products: 19.3 us -> 2.81 us
  between operations: 15 us -> 1.24 us
  other arithmetic: 6.98 us -> 10.8 us
    pallas_call x0 -> x1, Pallas kernels: none -> 108 us  [run_ring(): pl.pallas_call(functools.partial(expert_ring, steps, slots), out_shape=(j...]
    all_gather x1 -> x0, waiting for transfers between devices: 38.5 us -> none  [deliver(): lax.all_gather(owned_rows, 'seq', axis=1, tiled=True)]
    all_gather x1 -> x0, blocking collectives: 33.3 us -> none  [deliver(): lax.all_gather(owned_gates, 'seq', axis=1, tiled=True)]
    slice x1 -> x2, local copies, waits for them, and re-layouts: 34.7 us -> 1.95 us  [the longest x1 1.85 us: per_device(): owned[1]]
    psum x1 -> x0, blocking collectives: 24.7 us -> none  [per_device(): every_term = lax.psum(gate_terms, 'seq')]
    all_to_all x2 -> x1, starting transfers between devices: 30.7 us -> 10.9 us  [per_device(): lax.all_to_all(back, 'exp', split_axis=0, concat_axis=0, tiled=True)]
    another operation x6 -> x3, local copies, waits for them, and re-layouts: 18.3 us -> 0.73 us  [per_device(): jnp.stack([token_buffer, cot_buffer]).astype(BF16)]
    dot_general x12 -> x6, matrix products: 17.9 us -> 1.39 us  [the longest x2 0.45 us: front(): jnp.einsum('btd,de->bte', normed, router.astype(F32), precision=highest)]
  transfers between devices with their start and end apart: 4 -> 1, of which waited for: 4 -> 1; matrix products, arithmetic and copies ran while one was open for 6% -> 4% of each run, Pallas kernels for 0% -> 0%
where the time goes in v1:
time: 192 us; the launch traced here: 191 us
  Pallas kernels  108 us (56%)
  local copies, waits for them, and re-layouts  35.7 us (19%)
  blocking collectives  19.7 us (10%)
  starting transfers between devices  10.9 us (6%)
  other arithmetic  10.8 us (6%)
  matrix products  2.81 us (1%)
    pallas_call x1, Pallas kernels, run_ring(): pl.pallas_call(functools.partial(expert_ring, steps, slots), out_shape=(j...  108 us
    all_to_all x1, blocking collectives, per_device(): lax.all_to_all(row_buffer, 'exp', split_axis=1, concat_axis=1, tiled=True)  19.7 us
    unnamed x95, local copies, waits for them, and re-layouts  12.6 us
    all_to_all x1, starting transfers between devices, per_device(): lax.all_to_all(back, 'exp', split_axis=0, concat_axis=0, tiled=True)  10.9 us
  transfers between devices with their start and end apart: 1, of which 1 were waited for; matrix products, arithmetic and copies ran while one was open for 4% of the time, Pallas kernels for 0%

profile of v1, /device:TPU:1, one launch (start us, length us, event | category | flops | bytes accessed | tf_op | source)
XLA Modules:
  0.0 191.0 jit_solution(10887073847113996355)
XLA Ops:
  0.7 1.1 reshape.665
  5.7 0.8 reduce_sum.182
  9.2 1.1 fusion.6
  14.4 19.7 %all_to_all.10 = bf16[2,32,3,1024]{3,0,2,1:T(2,128)(2,1)S(1)} all-to-all(bf16[2,32,3,1024]{3,0,2,1:T(2,128)(2,1)S(1)} %copy.115), channel_id=1, replica_groups=mesh['seq'=16,'exp'=32] {'exp'}, dimensions={1} | all-to-all | bytes 786432 | tf_op jit(solution)/shard_map/all_to_all | solution.py:359
  34.1 1.8 slice_reduce_fusion
  37.0 1.0 copy-done.2
  38.1 108.3 %shard_map.103 = (f32[1024,256]{1,0:T(8,128)S(1)}, f32[256,1024]{1,0:T(8,128)S(1)}, bf16[96,1024]{1,0:T(8,128)(2,1)S(1)}, f32[8,128]{1,0:T(8,128)S(1)}) custom-call(bf16[96,1024]{1,0:T(8,128)(2,1)S(1)} %squeeze.26.x_ref, bf16[96,1024]{1,0:T(8,128)(2,1)S(1)} %squeeze.27.c_ref, bf16[1024,256]{1,0:T(8,128)(2,1)S(1)} %bitcast.105, bf16[256,1024]{1,0:T(8,128)(2,1)S(1)} %bitcast.106), custom_call_target="tpu_custom_call" | custom-call | tf_op jit(solution)/shard_map/pallas_call | solution.py:291
  146.5 0.8 reshape.669
  147.3 10.9 %all-to-all-start.1 = ((bf16[32,3,1152]{2,1,0:T(4,128)(2,1)}), bf16[32,3,1152]{2,1,0:T(4,128)(2,1)}, u32[]{:S(2)}, u32[]{:S(2)}) async-start(bf16[32,3,1152]{2,1,0:T(4,128)(2,1)} %reshape.669), calls=%async_computation.1 | async-start | bytes 589824 | tf_op jit(solution)/shard_map/all_to_all | solution.py:366
  162.1 0.8 copy.117
  162.9 1.2 broadcast_in_dim.101
  164.2 1.0 mul.434
  165.8 1.6 all-to-all-done.1
  167.4 1.1 reshape.670
  173.3 1.1 multiply_reduce_fusion.1
  176.0 1.0 broadcast_in_dim.97
  177.0 2.1 %broadcast_in_dim.98 = f32[1,128,1024]{2,1,0:T(8,128)} reshape(f32[32,4,1024]{2,1,0:T(4,128)} %broadcast_in_dim.97) | data formatting | bytes 1048576 | tf_op jit(solution)/shard_map/transpose(jvp())/broadcast_in_dim | solution.py:46
  179.1 2.1 %multiply_reduce_fusion.4 = (f32[128]{0:T(128)S(1)}, f32[128]{0:T(128)}) fusion(f32[1,128,1024]{2,1,0:T(8,128)} %mul.434, f32[1,128,1024]{2,1,0:T(8,128)S(1)} %copy-done.8, f32[1,128,1024]{2,1,0:T(8,128)} %broadcast_in_dim.98, f32[128]{0:T(128)S(1)} %copy-done.37, f32[128]{0:T(128)S(1)} %copy-done.36, f32[128]{0:T(128)S(1)} %copy-done.35, ...), kind=kLoop, calls=%fused_computation.15 | loop fusion | flops 1572608 | bytes 1838592 | tf_op jit(solution)/shard_map/transpose(jvp())/reduce_sum | solution.py:41
  182.6 1.5 multiply_add_fusion.1
  184.6 1.1 broadcast_in_dim.107
  185.7 1.5 broadcast_in_dim.108
  188.3 0.8 convert_element_type.54
  189.0 1.0 copy.142
  190.0 1.0 copy.143
  (161 shorter events, 25.4 us)
Async XLA Ops:
  0.6 10.4 %copy-start = (bf16[1024,32]{0,1:T(8,128)(2,1)S(1)}, bf16[1024,32]{0,1:T(8,128)(2,1)}, u32[]{:S(2)}) copy-start(bf16[1024,32]{0,1:T(8,128)(2,1)} %param.11) | copy-start | bytes 196612
  0.6 1.1 copy-start.3
  3.7 8.3 %copy-start.33 = (s32[32,2]{0,1:T(2,128)}, s32[32,2]{0,1:T(2,128)S(1)}, u32[]{:S(2)}) copy-start(s32[32,2]{0,1:T(2,128)S(1)} %multiply_add_fusion.2) | copy-start | bytes 772
  5.5 3.7 %copy-start.9 = (f32[32,1024]{1,0:T(8,128)}, f32[32,1024]{1,0:T(8,128)S(1)}, u32[]{:S(2)}) copy-start(f32[32,1024]{1,0:T(8,128)S(1)} %broadcast_multiply_fusion.1) | copy-start | bytes 393220
  5.7 2.5 %copy-start.31 = (f32[32]{0:T(128)}, f32[32]{0:T(128)S(1)}, u32[]{:S(2)}) copy-start(f32[32]{0:T(128)S(1)} %convolution_bitcast_fusion) | copy-start | bytes 388
  6.6 1.1 copy-start.6
  12.2 0.8 copy-start.12
  36.0 1.0 copy-start.1
  37.0 1.0 copy-start.2
  146.5 15.6 %copy-start.7 = (f32[32,2,1024]{2,1,0:T(2,128)S(1)}, f32[32,2,1024]{2,1,0:T(2,128)}, u32[]{:S(2)}) copy-start(f32[32,2,1024]{2,1,0:T(2,128)} %copy-done.6) | copy-start | bytes 786436
  147.3 15.6 %copy-start.5 = (f32[32,2,2,1024]{3,2,1,0:T(2,128)S(1)}, f32[32,2,2,1024]{3,2,1,0:T(2,128)}, u32[]{:S(2)}) copy-start(f32[32,2,2,1024]{3,2,1,0:T(2,128)} %copy-done.4) | copy-start | bytes 1572868
  147.3 20.1 %all-to-all-start.1 = ((bf16[32,3,1152]{2,1,0:T(4,128)(2,1)}), bf16[32,3,1152]{2,1,0:T(4,128)(2,1)}, u32[]{:S(2)}, u32[]{:S(2)}) async-start(bf16[32,3,1152]{2,1,0:T(4,128)(2,1)} %reshape.669), calls=%async_computation.1 | async-start | bytes 589824 | tf_op jit(solution)/shard_map/all_to_all | solution.py:366
  162.9 1.2 copy-start.10
  164.2 1.0 copy-start.22
  171.6 0.9 copy-start.13
  173.2 1.2 copy-start.11
  173.2 1.1 copy-start.30
  176.9 2.1 %copy-start.8 = (f32[1,128,1024]{2,1,0:T(8,128)S(1)}, f32[1,128,1024]{2,1,0:T(8,128)}, u32[]{:S(2)}) copy-start(f32[1,128,1024]{2,1,0:T(8,128)} %broadcast_in_dim.101) | copy-start | bytes 1572868
  176.9 2.1 %copy-start.35 = (f32[128]{0:T(128)S(1)}, f32[128]{0:T(128)}, u32[]{:S(2)}) copy-start(f32[128]{0:T(128)} %mul.425) | copy-start | bytes 1540
  176.9 2.1 %copy-start.36 = (f32[128]{0:T(128)S(1)}, f32[128]{0:T(128)}, u32[]{:S(2)}) copy-start(f32[128]{0:T(128)} %mul.428) | copy-start | bytes 1540
  176.9 2.1 %copy-start.37 = (f32[128]{0:T(128)S(1)}, f32[128]{0:T(128)}, u32[]{:S(2)}) copy-start(f32[128]{0:T(128)} %mul.431) | copy-start | bytes 1540
  176.9 2.1 %copy-start.38 = (f32[128]{0:T(128)S(1)}, f32[128]{0:T(128)}, u32[]{:S(2)}) copy-start(f32[128]{0:T(128)} %div.140) | copy-start | bytes 1540
  177.0 2.1 %copy-start.39 = (f32[128]{0:T(128)S(1)}, f32[128]{0:T(128)}, u32[]{:S(2)}) copy-start(f32[128]{0:T(128)} %mul.422) | copy-start | bytes 1540
  179.1 5.2 %copy-start.19 = (f32[1024]{0:T(1024)S(1)}, f32[1024]{0:T(1024)}, u32[]{:S(2)}) copy-start(f32[1024]{0:T(1024)} %param.9) | copy-start | bytes 12292
  (23 other events, 15.6 us)

commit v2 on v1

v2 whole, which is shorter than its diff:
```python
import functools

import jax
import jax.numpy as jnp
from jax import lax
from jax.experimental import pallas as pl
from jax.experimental.pallas import tpu as pltpu
from jax.sharding import PartitionSpec as P

SQRT_HALF = 0.7071067811865476
INV_ROOT_TWO_PI = 0.3989422804014327
MESH = pl.DeviceIdType.MESH
LANES = 128
SPLIT = 48
CAP = 3
GROUP = 16
ROWS = (((0,), (0,)), ((), ()))
COLS = (((1,), (1,)), ((), ()))
F32 = jnp.float32
BF16 = jnp.bfloat16


def pieces(value, count):
    out = []
    for _ in range(count):
        part = value.astype(BF16)
        out.append(part)
        value = value - part.astype(F32)
    return out


def stacked(value):
    parts = [value[:, at : at + LANES] for at in range(0, value.shape[1], LANES)]
    return jnp.concatenate(parts, axis=0)


def unstacked(value, rows):
    parts = [value[at : at + rows, :] for at in range(0, value.shape[0], rows)]
    return jnp.concatenate(parts, axis=1)


def total(value):
    return jnp.sum(value, axis=1, keepdims=True)


def iota(shape, dim):
    return lax.broadcasted_iota(jnp.int32, shape, dim)


def onehot(mask):
    return mask.astype(F32).astype(BF16)


def block_step(
    steps,
    peers,
    emb_hbm,
    score_ref,
    gain_ref,
    router_ref,
    routes_ref,
    win_hbm,
    wout_hbm,
    cot_hbm,
    gemb_ref,
    gin_ref,
    gout_ref,
    emb_ref,
    cot_ref,
    win_ref,
    wout_ref,
    value_ref,
    token_ref,
    send_ref,
    recv_ref,
    bsend_ref,
    brecv_ref,
    sel_ref,
    pick_ref,
    xs,
    cs,
    hid,
    hgrad,
    part,
    gpart,
    take,
    give,
    gtake,
    ggive,
    in_sem,
    fx_send,
    fx_recv,
    bx_send,
    bx_recv,
    ag_send,
    ag_recv,
    rs_send,
    rs_recv,
    rg_send,
    rg_recv,
):
    me = lax.axis_index("seq")
    mine = lax.axis_index("exp")
    half = steps // 2
    right = lax.rem(me + 1, steps)
    left = lax.rem(me + steps - 1, steps)
    tokens_here, width = cot_ref.shape
    slots = peers * CAP
    parts = width // LANES
    block = width // half

    loads = [
        pltpu.make_async_copy(src, dst, in_sem.at[at])
        for at, (src, dst) in enumerate(
            ((emb_hbm, emb_ref), (cot_hbm, cot_ref), (win_hbm, win_ref), (wout_hbm, wout_ref))
        )
    ]
    for load in loads:
        load.start()

    barrier = pltpu.get_barrier_semaphore()
    for peer in (left, right):
        pl.semaphore_signal(barrier, inc=1, device_id={"seq": peer}, device_id_type=MESH)

    def greet(k, carry):
        pl.semaphore_signal(
            barrier, inc=1, device_id={"exp": lax.rem(mine + k, peers)}, device_id_type=MESH
        )
        return carry

    lax.fori_loop(1, peers, greet, 0)

    loads[0].wait()
    loads[1].wait()
    count = 4 * tokens_here
    order = iota((count, count), 0)
    place = iota((count, count), 1)
    shuffle = onehot(place == lax.rem(order, tokens_here) * 4 + order // tokens_here)
    value_ref[...] = jnp.dot(shuffle, emb_ref[...], preferred_element_type=F32)
    values = [value_ref[pl.ds(i * tokens_here, tokens_here), :] for i in range(4)]
    weight = score_ref[...]
    scores = [total(v * weight) for v in values]
    pair = [0.5 * (scores[0] + scores[1]), 0.5 * (scores[2] + scores[3])]
    quad = 0.5 * (pair[0] + pair[1])
    shares = []
    for i in range(4):
        three = (scores[i], pair[i // 2], quad)
        top = jnp.maximum(jnp.maximum(three[0], three[1]), three[2])
        raised = [jnp.exp(s - top) for s in three]
        bottom = raised[0] + raised[1] + raised[2]
        shares.append([r / bottom for r in raised])
    pair_share = [shares[2 * h][1] + shares[2 * h + 1][1] for h in range(2)]
    quad_share = shares[0][2] + shares[1][2] + shares[2][2] + shares[3][2]
    mix = [
        0.25 * (shares[i][0] + 0.5 * pair_share[i // 2] + 0.25 * quad_share) for i in range(4)
    ]
    token = mix[0] * values[0] + mix[1] * values[1] + mix[2] * values[2] + mix[3] * values[3]
    token_ref[...] = token
    scale = lax.rsqrt(total(token * token) * (1.0 / width) + 1e-06)
    normed = token * scale * gain_ref[...]
    sent = normed.astype(BF16)
    router = router_ref[...]
    logits = jnp.zeros((tokens_here, peers), F32)
    for piece in pieces(normed, 3):
        logits = logits + jnp.dot(piece, router, preferred_element_type=F32)
    lane = iota((tokens_here, peers), 1)
    chosen = [lane == routes_ref[:, k : k + 1] for k in range(2)]
    picked = [total(jnp.where(hit, logits, 0.0)) for hit in chosen]
    sigmoids = [1.0 / (1.0 + jnp.exp(-v)) for v in picked]
    gates = [s / (sigmoids[0] + sigmoids[1]) for s in sigmoids]
    named = onehot(chosen[0]) + onehot(chosen[1])
    before = onehot(iota((tokens_here, tokens_here), 1) < iota((tokens_here, tokens_here), 0))
    earlier = jnp.dot(before, named, preferred_element_type=F32)
    spots = [total(jnp.where(hit, earlier, 0.0)).astype(jnp.int32) for hit in chosen]
    codes = [routes_ref[:, k : k + 1] * 4 + spots[k] for k in range(2)]

    tall = parts * tokens_here
    long = peers * GROUP
    column = iota((tall, long), 1)
    expert = column // GROUP
    inner = lax.rem(column, GROUP)
    upper = inner // 8
    piece_at = lax.rem(inner, 8)
    row_piece = iota((tall, 1), 0) // tokens_here
    row_codes = [jnp.concatenate([code] * parts, axis=0) * 8 + row_piece for code in codes]
    row_gates = [jnp.concatenate([gate] * parts, axis=0) for gate in gates]
    base = expert * 32 + piece_at
    wanted = (
        base + upper * 8,
        jnp.where(upper == 0, base + 16, -1),
        jnp.where(upper == 1, base, -1),
        base + 8 + upper * 8,
    )
    for at in range(2):
        hit = jnp.where(row_codes[0] == wanted[at], 1.0, 0.0)
        hit = hit + jnp.where(row_codes[1] == wanted[at], 1.0, 0.0)
        sel_ref[at] = hit.astype(BF16)
    sent_tall = stacked(sent)
    cot_tall = stacked(cot_ref[...])
    own = []
    for at in range(2):
        own.append(lax.dot_general(sel_ref[at], sent_tall, ROWS, preferred_element_type=F32))
    for at in range(2, 4):
        gated = jnp.where(row_codes[0] == wanted[at], row_gates[0], 0.0)
        gated = gated + jnp.where(row_codes[1] == wanted[at], row_gates[1], 0.0)
        high, low = pieces(gated, 2)
        one = lax.dot_general(high, cot_tall, ROWS, preferred_element_type=F32)
        own.append(one + lax.dot_general(low, cot_tall, ROWS, preferred_element_type=F32))
    send_ref[:, 0:LANES] = own[0].astype(BF16)
    send_ref[:, LANES : 2 * LANES] = (own[1] + own[2]).astype(BF16)
    send_ref[:, 2 * LANES : 3 * LANES] = own[3].astype(BF16)

    pl.semaphore_wait(barrier, peers + 1)

    def group_rows(index):
        return pl.ds(pl.multiple_of(index * GROUP, GROUP), GROUP)

    def exchange(k, src_ref, dst_ref, send_sem, recv_sem):
        peer = lax.rem(mine + k, peers)
        return pltpu.make_async_remote_copy(
            src_ref=src_ref.at[group_rows(peer)],
            dst_ref=dst_ref.at[group_rows(mine)],
            send_sem=send_sem.at[k],
            recv_sem=recv_sem.at[k],
            device_id={"exp": peer},
            device_id_type=MESH,
        )

    def arrived(k, src_ref, dst_ref, send_sem, recv_sem):
        peer = lax.rem(mine + peers - k, peers)
        return pltpu.make_async_remote_copy(
            src_ref=src_ref.at[group_rows(peer)],
            dst_ref=dst_ref.at[group_rows(peer)],
            send_sem=send_sem.at[k],
            recv_sem=recv_sem.at[k],
            device_id={"exp": peer},
            device_id_type=MESH,
        )

    def exchange_start(*refs):
        def start(k, carry):
            exchange(k, *refs).start()
            return carry

        lax.fori_loop(1, peers, start, 0)
        refs[1][group_rows(mine), :] = refs[0][group_rows(mine), :]

    def exchange_wait(*refs):
        def wait(k, carry):
            arrived(k, *refs).wait_recv()
            return carry

        lax.fori_loop(1, peers, wait, 0)

    def exchange_end(*refs):
        def wait(k, carry):
            exchange(k, *refs).wait_send()
            return carry

        lax.fori_loop(1, peers, wait, 0)

    forward = (send_ref, recv_ref, fx_send, fx_recv)
    backward = (bsend_ref, brecv_ref, bx_send, bx_recv)
    exchange_start(*forward)

    near = 16
    few = near * CAP
    deep = parts * few
    wide = near * GROUP
    row = iota((deep, wide), 0)
    slot = lax.rem(row, few)
    inner = lax.rem(iota((deep, wide), 1), GROUP)
    same = (slot // CAP == iota((deep, wide), 1) // GROUP) & (lax.rem(inner, 8) == row // few)
    spot = lax.rem(slot, CAP)
    upper = inner // 8
    pick_ref[0] = onehot(same & (spot == upper))
    pick_ref[1] = onehot(same & (spot == 2) & (upper == 0))
    pick_ref[2] = onehot(same & (spot == 0) & (upper == 1))
    pick_ref[3] = onehot(same & (spot == 1 + upper))
    gpart[...] = jnp.zeros_like(gpart)

    def rows_of(index, start=0, size=slots):
        return pl.ds(pl.multiple_of(index * slots + start, 16), size)

    def source(way, j):
        return lax.rem(me - j + steps, steps) if way == 0 else lax.rem(me + j, steps)

    def gather(way, j, sub):
        buf = cs if sub else xs
        at = rows_of(source(way, j))
        return pltpu.make_async_remote_copy(
            src_ref=buf.at[at],
            dst_ref=buf.at[at],
            send_sem=ag_send.at[way, j, sub],
            recv_sem=ag_recv.at[way, j, sub],
            device_id={"seq": left if way else right},
            device_id_type=MESH,
        )

    def arrival(way, j, sub):
        buf = cs if sub else xs
        at = rows_of(source(way, j + 1))
        return pltpu.make_async_remote_copy(
            src_ref=buf.at[at],
            dst_ref=buf.at[at],
            send_sem=ag_send.at[way, j, sub],
            recv_sem=ag_recv.at[way, j, sub],
            device_id={"seq": left if way else right},
            device_id_type=MESH,
        )

    def target(way, s):
        return lax.rem(me + half - s, steps) if way == 0 else lax.rem(me + half + s, steps)

    def scatter(way, s, sub, direct=False):
        at = way * half + s
        here = rows_of(at, sub * SPLIT, SPLIT)
        src = part.at[rows_of(target(way, s), sub * SPLIT, SPLIT)] if direct else give.at[here]
        return pltpu.make_async_remote_copy(
            src_ref=src,
            dst_ref=take.at[here],
            send_sem=rs_send.at[way, s, sub],
            recv_sem=rs_recv.at[way, s, sub],
            device_id={"seq": left if way else right},
            device_id_type=MESH,
        )

    def scatter_gate(way, s, direct=False):
        at = way * half + s
        src = gpart.at[target(way, s)] if direct else ggive.at[at]
        return pltpu.make_async_remote_copy(
            src_ref=src,
            dst_ref=gtake.at[at],
            send_sem=rg_send.at[way, s],
            recv_sem=rg_recv.at[way, s],
            device_id={"seq": left if way else right},
            device_id_type=MESH,
        )

    def compute(index):
        at = rows_of(index)
        pre = jnp.dot(xs[at, :], win_ref[...], preferred_element_type=F32)
        up = lax.dot_general(cs[at, :], wout_ref[...], COLS, preferred_element_type=F32)
        cdf = 0.5 * (1.0 + lax.erf(pre * SQRT_HALF))
        pdf = INV_ROOT_TWO_PI * jnp.exp(-0.5 * pre * pre)
        hidden = pre * cdf
        hg = (up * (cdf + pre * pdf)).astype(BF16)
        hid[at, :] = hidden.astype(BF16)
        hgrad[at, :] = hg
        part[at, :] = lax.dot_general(
            hg, win_ref[...], COLS, preferred_element_type=F32
        ).astype(BF16)
        high, low = pieces(hidden * up, 2)
        ones = jnp.ones((8, high.shape[1]), BF16)
        terms = lax.dot_general(ones, high, COLS, preferred_element_type=F32)
        terms = terms + lax.dot_general(ones, low, COLS, preferred_element_type=F32)
        gpart[index, :, 0:slots] = terms

    exchange_wait(*forward)
    for sub, buf in enumerate((xs, cs)):
        for near_at in range(peers // near):
            here = recv_ref[pl.ds(near_at * wide, wide), :]
            lanes = sub * LANES
            one = jnp.dot(
                pick_ref[2 * sub], here[:, lanes : lanes + LANES], preferred_element_type=F32
            )
            two = jnp.dot(
                pick_ref[2 * sub + 1],
                here[:, lanes + LANES : lanes + 2 * LANES],
                preferred_element_type=F32,
            )
            buf[rows_of(me, near_at * few, few), :] = unstacked((one + two).astype(BF16), few)
        for way in range(2):
            gather(way, 0, sub).start()
    loads[2].wait()
    loads[3].wait()
    compute(me)

    def ring_step(j, carry):
        for sub in range(2):
            for way in range(2):
                arrival(way, j - 1, sub).wait_recv()
                gather(way, j, sub).start()
        compute(source(0, j))
        compute(source(1, j))
        return carry

    lax.fori_loop(1, half - 1, ring_step, 0)

    last = half - 1
    for sub in range(2):
        for way in range(2):
            arrival(way, last - 1, sub).wait_recv()
            if sub == way:
                gather(way, last, sub).start()
    compute(source(0, last))
    compute(source(1, last))
    scatter(0, 1, 1, direct=True).start()
    scatter(1, 1, 0, direct=True).start()
    scatter_gate(1, 1, direct=True).start()
    arrival(0, last, 0).wait_recv()
    arrival(1, last, 1).wait_recv()
    compute(source(0, half))

    def weights(s):
        span = pl.ds(pl.multiple_of(s * block, LANES), block)
        gin_ref[span, :] = lax.dot_general(
            xs[:, span], hgrad[...], ROWS, preferred_element_type=F32
        )
        gout_ref[:, span] = lax.dot_general(
            hid[...], cs[:, span], ROWS, preferred_element_type=F32
        )

    def merge(way, s, sub):
        at = way * half + s
        ours = part[rows_of(target(way, s), sub * SPLIT, SPLIT), :].astype(F32)
        came = take[rows_of(at - 1, sub * SPLIT, SPLIT), :].astype(F32)
        give[rows_of(at, sub * SPLIT, SPLIT), :] = (ours + came).astype(BF16)

    scatter(0, 0, 0, direct=True).start()
    scatter(1, 0, 1, direct=True).start()
    scatter_gate(0, 0, direct=True).start()
    weights(0)
    scatter(0, 0, 0, direct=True).wait_recv()
    merge(0, 1, 0)
    scatter(0, 1, 0).start()
    scatter(1, 0, 1, direct=True).wait_recv()
    merge(1, 1, 1)
    scatter(1, 1, 1).start()
    scatter_gate(0, 0, direct=True).wait_recv()
    ggive[1] = gpart[target(0, 1)] + gtake[0]
    scatter_gate(0, 1).start()
    weights(1)

    def scatter_step(s, carry):
        for order in range(2):
            for way in range(2):
                sub = (1 - order) if way == 0 else order
                scatter(way, s - 1, sub).wait_recv()
                merge(way, s, sub)
                scatter(way, s, sub).start()
        for way in range(2):
            scatter_gate(way, s - 1).wait_recv()
            at = way * half + s
            ggive[at] = gpart[target(way, s)] + gtake[at - 1]
            scatter_gate(way, s).start()
        weights(s)
        return carry

    lax.fori_loop(2, half, scatter_step, 0)

    summed = []
    for sub in range(2):
        whole = part[rows_of(me, sub * SPLIT, SPLIT), :].astype(F32)
        for way in range(2):
            scatter(way, last, sub).wait_recv()
            whole = whole + take[rows_of(way * half + last, sub * SPLIT, SPLIT), :].astype(F32)
        summed.append(whole.astype(BF16))
    terms = gpart[me]
    for way in range(2):
        scatter_gate(way, last).wait_recv()
        terms = terms + gtake[way * half + last]

    for near_at in range(peers // near):
        tall_rows = stacked(summed[near_at])
        here = pl.ds(near_at * wide, wide)
        for at in range(2):
            bsend_ref[here, pl.ds(at * LANES, LANES)] = lax.dot_general(
                pick_ref[at], tall_rows, ROWS, preferred_element_type=F32
            ).astype(BF16)
    row = iota((long, LANES), 0)
    column = iota((long, LANES), 1)
    fits = (column // CAP == row // GROUP) & (
        lax.rem(row, GROUP) == 8 + lax.rem(column, CAP)
    )
    spread = total(jnp.where(fits & (column < slots), terms[0:1, :], 0.0))
    high, low = pieces(spread, 2)
    two = jnp.where(column < LANES // 2, high.astype(F32), low.astype(F32))
    kept = bsend_ref[:, LANES : 2 * LANES].astype(F32)
    bsend_ref[:, LANES : 2 * LANES] = (kept + two).astype(BF16)
    exchange_start(*backward)
    exchange_end(*forward)
    for way in range(2):
        for s in range(half):
            for sub in range(2):
                if s < last or sub == way:
                    gather(way, s, sub).wait_send()
                if s >= 1 or sub == way:
                    scatter(way, s, sub).wait_send()
            if s >= 1 or way == 0:
                scatter_gate(way, s).wait_send()
    exchange_wait(*backward)

    first = brecv_ref[:, 0:LANES]
    second = brecv_ref[:, LANES : 2 * LANES]
    back = jnp.dot(sel_ref[0], first, preferred_element_type=F32)
    back = back + jnp.dot(sel_ref[1], second, preferred_element_type=F32)
    normed_grad = unstacked(back, tokens_here)
    column = iota((tokens_here, long), 1)
    scaled = []
    for k in range(2):
        at = routes_ref[:, k : k + 1] * GROUP + 8 + spots[k]
        found = jnp.dot(onehot(column == at), second, preferred_element_type=F32)
        scaled.append(found[:, 0:1] + found[:, LANES // 2 : LANES // 2 + 1])
    both = scaled[0] + scaled[1]
    logit_grad = jnp.zeros((tokens_here, peers), F32)
    for k in range(2):
        one = (1.0 - sigmoids[k]) * (scaled[k] - gates[k] * both)
        logit_grad = logit_grad + jnp.where(chosen[k], one, 0.0)
    for piece in pieces(logit_grad, 3):
        normed_grad = normed_grad + lax.dot_general(
            piece, router, COLS, preferred_element_type=F32
        )
    token = token_ref[...]
    inner_grad = normed_grad * gain_ref[...]
    slope = total(inner_grad * token) * (scale * scale * scale * (1.0 / width))
    token_grad = cot_ref[...].astype(F32) + inner_grad * scale - token * slope
    values = [value_ref[pl.ds(i * tokens_here, tokens_here), :] for i in range(4)]
    hits = [total(token_grad * v) for v in values]
    pair_hit = [hits[0] + hits[1], hits[2] + hits[3]]
    quad_hit = pair_hit[0] + pair_hit[1]
    score_grads = []
    for i in range(4):
        grads = (0.25 * hits[i], 0.125 * pair_hit[i // 2], 0.0625 * quad_hit)
        mean = sum(a * g for a, g in zip(shares[i], grads))
        score_grads.append([a * (g - mean) for a, g in zip(shares[i], grads)])
    pair_grad = [score_grads[2 * h][1] + score_grads[2 * h + 1][1] for h in range(2)]
    quad_grad = sum(g[2] for g in score_grads)
    result = []
    for i in range(4):
        own_grad = score_grads[i][0] + 0.5 * pair_grad[i // 2] + 0.25 * quad_grad
        result.append((mix[i] * token_grad + own_grad * weight).astype(BF16))
    shuffle = onehot(order == lax.rem(place, tokens_here) * 4 + place // tokens_here)
    gemb_ref[...] = jnp.dot(
        shuffle, jnp.concatenate(result, axis=0), preferred_element_type=F32
    ).astype(BF16)
    exchange_end(*backward)


def per_device(
    byte_embed, score_weight, norm_gain, router, routes, expert_in, expert_out, cotangent
):
    steps, peers = lax.axis_size("seq"), lax.axis_size("exp")
    count, width = byte_embed.shape[1:]
    hidden = expert_in.shape[2]
    tokens_here = routes.shape[1]
    half = steps // 2
    slots = peers * CAP
    long = peers * GROUP
    parts = width // LANES
    vmem = pl.BlockSpec(memory_space=pltpu.VMEM)
    hbm = pl.BlockSpec(memory_space=pl.ANY)
    dma = pltpu.SemaphoreType.DMA
    gemb, gin, gout = pl.pallas_call(
        functools.partial(block_step, steps, peers),
        out_shape=(
            jax.ShapeDtypeStruct((count, width), BF16),
            jax.ShapeDtypeStruct((width, hidden), F32),
            jax.ShapeDtypeStruct((hidden, width), F32),
        ),
        in_specs=[hbm, vmem, vmem, vmem, vmem, hbm, hbm, hbm],
        out_specs=(vmem,) * 3,
        scratch_shapes=[
            pltpu.VMEM((count, width), BF16),
            pltpu.VMEM((tokens_here, width), BF16),
            pltpu.VMEM((width, hidden), BF16),
            pltpu.VMEM((hidden, width), BF16),
            pltpu.VMEM((count, width), F32),
            pltpu.VMEM((tokens_here, width), F32),
            pltpu.VMEM((long, 3 * LANES), BF16),
            pltpu.VMEM((long, 3 * LANES), BF16),
            pltpu.VMEM((long, 2 * LANES), BF16),
            pltpu.VMEM((long, 2 * LANES), BF16),
            pltpu.VMEM((2, parts * tokens_here, long), BF16),
            pltpu.VMEM((4, parts * 16 * CAP, 16 * GROUP), BF16),
            pltpu.VMEM((steps * slots, width), BF16),
            pltpu.VMEM((steps * slots, width), BF16),
            pltpu.VMEM((steps * slots, hidden), BF16),
            pltpu.VMEM((steps * slots, hidden), BF16),
            pltpu.VMEM((steps * slots, width), BF16),
            pltpu.VMEM((steps, 8, LANES), F32),
            pltpu.VMEM((steps * slots, width), BF16),
            pltpu.VMEM((steps * slots, width), BF16),
            pltpu.VMEM((steps, 8, LANES), F32),
            pltpu.VMEM((steps, 8, LANES), F32),
            dma((4,)),
            dma((peers,)),
            dma((peers,)),
            dma((peers,)),
            dma((peers,)),
            dma((2, half, 2)),
            dma((2, half, 2)),
            dma((2, half, 2)),
            dma((2, half, 2)),
            dma((2, half)),
            dma((2, half)),
        ],
        compiler_params=pltpu.CompilerParams(
            collective_id=0, has_side_effects=True, vmem_limit_bytes=52 * 1024 * 1024
        ),
    )(
        byte_embed[0],
        score_weight[None],
        norm_gain[None],
        router,
        routes[0],
        expert_in[0],
        expert_out[0],
        cotangent[0],
    )
    return (gemb[None], gin[None], gout[None])


def solution(mesh):
    in_specs = (
        P("exp", "seq", None),
        P(),
        P(),
        P(),
        P("exp", "seq", None),
        P("exp", None, "seq"),
        P("exp", "seq", None),
        P("exp", "seq", None),
    )
    out_specs = (P("exp", "seq", None), P("exp", None, "seq"), P("exp", "seq", None))
    return jax.shard_map(
        per_device, mesh=mesh, in_specs=in_specs, out_specs=out_specs, check_vma=False
    )
```

time: 192 us -> 148 us (0.77)
  Pallas kernels: 108 us -> 139 us
  local copies, waits for them, and re-layouts: 35.7 us -> 7.96 us
  blocking collectives: 19.7 us -> 0 us
  starting transfers between devices: 10.9 us -> 0 us
  other arithmetic: 10.8 us -> 0 us
  matrix products: 2.81 us -> 0 us
    pallas_call x1, Pallas kernels: 108 us -> 139 us  [per_device(): pl.pallas_call(functools.partial(block_step, steps, peers), out_shape=(ja...]
    all_to_all x1 -> x0, blocking collectives: 19.7 us -> none  [per_device(): lax.all_to_all(row_buffer, 'exp', split_axis=1, concat_axis=1, tiled=True)]
    all_to_all x1 -> x0, starting transfers between devices: 10.9 us -> none  [per_device(): lax.all_to_all(back, 'exp', split_axis=0, concat_axis=0, tiled=True)]
    broadcast_in_dim x12 -> x0, local copies, waits for them, and re-layouts: 8.51 us -> none  [the longest x2 3.02 us: front(): tokens = blended.mean(axis=2)]
    reduce_sum x14 -> x0, other arithmetic: 6.47 us -> none  [the longest x1 2.1 us: front(): (weight_one[..., None] * quartets + weight_two[..., None] * pair_full + w...]
    unnamed x95 -> x18, local copies, waits for them, and re-layouts: 12.6 us -> 7.16 us
    reshape x6 -> x0, local copies, waits for them, and re-layouts: 3.76 us -> none  [the longest x1 1.15 us: per_device(): returned = returned.reshape(slots, width_model + LANES)]
    mul x6 -> x0, local copies, waits for them, and re-layouts: 3.7 us -> none  [the longest x3 1.79 us: front(): weight_four[..., None] * quad_mean[:, :, None, :]]
  transfers between devices with their start and end apart: 1 -> 0, of which waited for: 1 -> 0; matrix products, arithmetic and copies ran while one was open for 4% -> 0% of each run, Pallas kernels for 0% -> 0%
where the time goes in v2:
time: 148 us
  Pallas kernels  139 us (94%)
  local copies, waits for them, and re-layouts  7.96 us (5%)
    pallas_call x1, Pallas kernels, per_device(): pl.pallas_call(functools.partial(block_step, steps, peers), out_shape=(ja...  139 us
    unnamed x18, local copies, waits for them, and re-layouts  7.16 us

profile of v2, /device:TPU:1, one launch (start us, length us, event | category | flops | bytes accessed | tf_op | source)
XLA Modules:
  0.0 148.0 jit_solution(14673315405452481465)
XLA Ops:
  0.6 0.0 copy-start.2
  0.6 0.8 copy.12.routes_ref
  1.4 0.0 copy-start.3
  1.4 0.0 copy-start.4
  1.4 0.0 copy-start.5
  1.5 1.0 copy.11.router_ref
  2.5 0.0 copy-done.2
  2.5 0.0 copy-done.3
  2.5 0.0 copy-done.4
  2.5 0.0 copy-done.5
  2.5 0.0 copy-start
  2.5 1.0 copy-done
  3.6 0.0 copy-start.1
  3.6 1.0 copy-done.1
  4.6 139.4 %shard_map.103 = (bf16[128,1024]{1,0:T(8,128)(2,1)S(1)}, f32[1024,256]{1,0:T(8,128)}, f32[256,1024]{1,0:T(8,128)}) custom-call(bf16[128,1024]{1,0:T(8,128)(2,1)S(1)} %bitcast.12, f32[1,1024]{1,0:T(1,128)S(1)} %bitcast.15, f32[1,1024]{1,0:T(1,128)S(1)} %bitcast.16, bf16[1024,32]{1,0:T(8,128)(2,1)S(1)} %copy.11.router_ref, s32[32,2]{1,0:T(8,128)S(1)} %copy.12.routes_ref, ...), custom_call_target="tpu_custom_call" | custom-call | tf_op jit(solution)/shard_map/pallas_call | solution.py:554
  144.0 0.7 copy.16
  144.7 0.0 copy-start.6
  144.7 2.4 %copy.17 = f32[1,1024,256]{2,1,0:T(8,128)} copy(f32[1,1024,256]{2,1,0:T(8,128)} %bitcast.18) | data formatting | bytes 2097152
  147.1 0.0 copy-done.6
  147.1 1.0 copy.18
Async XLA Ops:
  0.6 1.9 %copy-start.2 = (bf16[1,128,1024]{2,1,0:T(8,128)(2,1)S(1)}, bf16[1,128,1024]{2,1,0:T(8,128)(2,1)}, u32[]{:S(2)}) copy-start(bf16[1,128,1024]{2,1,0:T(8,128)(2,1)} %param.8) | copy-start | bytes 786436
  1.4 1.1 copy-start.3
  1.4 1.1 copy-start.4
  1.4 1.1 copy-start.5
  2.5 1.0 copy-start
  3.6 1.0 copy-start.1
  144.7 2.4 %copy-start.6 = (f32[256,1024]{1,0:T(8,128)S(1)}, f32[256,1024]{1,0:T(8,128)}, u32[]{:S(2)}) copy-start(f32[256,1024]{1,0:T(8,128)} %get-tuple-element.8) | copy-start | bytes 3145732

commit v3 on v2

--- a/solution.py
+++ b/solution.py
@@ -12,6 +12,7 @@
 MESH = pl.DeviceIdType.MESH
 LANES = 128
 SPLIT = 48
+SPREAD = 3
 CAP = 3
 GROUP = 16
 ROWS = (((0,), (0,)), ((), ()))
@@ -55,10 +56,10 @@
     steps,
     peers,
     emb_hbm,
-    score_ref,
-    gain_ref,
-    router_ref,
-    routes_ref,
+    score_hbm,
+    gain_hbm,
+    router_hbm,
+    routes_hbm,
     win_hbm,
     wout_hbm,
     cot_hbm,
@@ -69,6 +70,10 @@
     cot_ref,
     win_ref,
     wout_ref,
+    score_ref,
+    gain_ref,
+    router_ref,
+    routes_ref,
     value_ref,
     token_ref,
     send_ref,
@@ -77,6 +82,10 @@
     brecv_ref,
     sel_ref,
     pick_ref,
+    spread_ref,
+    tb,
+    tsend,
+    trecv,
     xs,
     cs,
     hid,
@@ -92,6 +101,10 @@
     fx_recv,
     bx_send,
     bx_recv,
+    tb_send,
+    tb_recv,
+    tx_send,
+    tx_recv,
     ag_send,
     ag_recv,
     rs_send,
@@ -108,11 +121,25 @@
     slots = peers * CAP
     parts = width // LANES
     block = width // half
+    count_sub = slots // SPLIT
+    early = (tuple(range(count_sub // 2)), tuple(range(count_sub // 2, count_sub)))
+    fresh = early[::-1]
+    wide_cols = SPREAD * LANES
+    ring_cols = width - wide_cols
 
     loads = [
         pltpu.make_async_copy(src, dst, in_sem.at[at])
         for at, (src, dst) in enumerate(
-            ((emb_hbm, emb_ref), (cot_hbm, cot_ref), (win_hbm, win_ref), (wout_hbm, wout_ref))
+            (
+                (emb_hbm, emb_ref),
+                (score_hbm, score_ref),
+                (gain_hbm, gain_ref),
+                (routes_hbm, routes_ref),
+                (router_hbm, router_ref),
+                (cot_hbm, cot_ref),
+                (win_hbm, win_ref),
+                (wout_hbm, wout_ref),
+            )
         )
     ]
     for load in loads:
@@ -157,14 +184,21 @@
     token = mix[0] * values[0] + mix[1] * values[1] + mix[2] * values[2] + mix[3] * values[3]
     token_ref[...] = token
     scale = lax.rsqrt(total(token * token) * (1.0 / width) + 1e-06)
+    for load in loads[2:6]:
+        load.wait()
     normed = token * scale * gain_ref[...]
     sent = normed.astype(BF16)
     router = router_ref[...]
     logits = jnp.zeros((tokens_here, peers), F32)
     for piece in pieces(normed, 3):
-        logits = logits + jnp.dot(piece, router, preferred_element_type=F32)
+        logits = logits + lax.dot_general(piece, router, COLS, preferred_element_type=F32)
     lane = iota((tokens_here, peers), 1)
-    chosen = [lane == routes_ref[:, k : k + 1] for k in range(2)]
+    level = lane == iota((tokens_here, peers), 0)
+    named = routes_ref[...].astype(F32)
+    routes = [
+        total(jnp.where(level, named[k : k + 1, :], 0.0)).astype(jnp.int32) for k in range(2)
+    ]
+    chosen = [lane == routes[k] for k in range(2)]
     picked = [total(jnp.where(hit, logits, 0.0)) for hit in chosen]
     sigmoids = [1.0 / (1.0 + jnp.exp(-v)) for v in picked]
     gates = [s / (sigmoids[0] + sigmoids[1]) for s in sigmoids]
@@ -172,7 +206,7 @@
     before = onehot(iota((tokens_here, tokens_here), 1) < iota((tokens_here, tokens_here), 0))
     earlier = jnp.dot(before, named, preferred_element_type=F32)
     spots = [total(jnp.where(hit, earlier, 0.0)).astype(jnp.int32) for hit in chosen]
-    codes = [routes_ref[:, k : k + 1] * 4 + spots[k] for k in range(2)]
+    codes = [routes[k] * 4 + spots[k] for k in range(2)]
 
     tall = parts * tokens_here
     long = peers * GROUP
@@ -210,7 +244,117 @@
     send_ref[:, LANES : 2 * LANES] = (own[1] + own[2]).astype(BF16)
     send_ref[:, 2 * LANES : 3 * LANES] = own[3].astype(BF16)
 
+    meta = jnp.zeros((tokens_here, LANES), F32)
+    lane = iota((tokens_here, LANES), 1)
+    for k in range(2):
+        high, low = pieces(gates[k], 2)
+        for at, column in enumerate((codes[k].astype(F32), high.astype(F32), low.astype(F32))):
+            meta = jnp.where(lane == 2 * at + k, column, meta)
+
+    def token_rows(index):
+        return pl.ds(pl.multiple_of(index * tokens_here, tokens_here), tokens_here)
+
+    tb[token_rows(me), 0:LANES] = meta.astype(BF16)
+    tb[token_rows(me), LANES : LANES + wide_cols] = sent[:, ring_cols:]
+    tb[token_rows(me), LANES + wide_cols :] = cot_ref[:, ring_cols:]
+
+    def source(way, j):
+        return lax.rem(me - j + steps, steps) if way == 0 else lax.rem(me + j, steps)
+
+    def token_copy(way, j, index):
+        cols = pl.ds(0, LANES + 2 * wide_cols)
+        if isinstance(j, int) and j == half - 1:
+            cols = pl.ds(LANES + wide_cols, wide_cols) if way else pl.ds(0, LANES + wide_cols)
+        here = tb.at[token_rows(index), cols]
+        return pltpu.make_async_remote_copy(
+            src_ref=here,
+            dst_ref=here,
+            send_sem=tb_send.at[way, j],
+            recv_sem=tb_recv.at[way, j],
+            device_id={"seq": left if way else right},
+            device_id_type=MESH,
+        )
+
+    def token_send(way, j):
+        return token_copy(way, j, source(way, j))
+
+    def token_arrival(way, j):
+        return token_copy(way, j, source(way, j + 1))
+
+    def spread_rows(j, start=0, size=long):
+        return pl.ds(pl.multiple_of((j - 1) * long + start, 16), size)
+
+    def spread_copy(j, k):
+        peer = lax.rem(mine + k, peers)
+        return pltpu.make_async_remote_copy(
+            src_ref=tsend.at[spread_rows(j, peer * GROUP, GROUP)],
+            dst_ref=trecv.at[spread_rows(j, mine * GROUP, GROUP)],
+            send_sem=tx_send.at[j - 1],
+            recv_sem=tx_recv.at[j - 1],
+            device_id={"exp": peer},
+            device_id_type=MESH,
+        )
+
+    def spread_all(j):
+        size = (peers - 1) * GROUP
+        return pltpu.make_async_remote_copy(
+            src_ref=tsend.at[spread_rows(j, 0, size)],
+            dst_ref=trecv.at[spread_rows(j, 0, size)],
+            send_sem=tx_send.at[j - 1],
+            recv_sem=tx_recv.at[j - 1],
+            device_id={"exp": lax.rem(mine + 1, peers)},
+            device_id_type=MESH,
+        )
+
+    def choose(index, offset):
+        block = tb[token_rows(index), :]
+        meta = block[:, 0:LANES].astype(F32)
+        column = iota((tokens_here, long), 1)
+        row = lax.rem(column, GROUP) - offset
+        base = (column // GROUP) * 4
+        for_x = jnp.where((row >= 0) & (row < CAP), base + row, -1).astype(F32)
+        for_c = jnp.where((row >= CAP) & (row < 2 * CAP), base + row - CAP, -1).astype(F32)
+        found = high = low = jnp.zeros((tokens_here, long), F32)
+        for k in range(2):
+            code = meta[:, k : k + 1]
+            found = found + jnp.where(code == for_x, 1.0, 0.0)
+            high = high + jnp.where(code == for_c, meta[:, 2 + k : 3 + k], 0.0)
+            low = low + jnp.where(code == for_c, meta[:, 4 + k : 5 + k], 0.0)
+        cot = block[:, LANES + wide_cols :]
+        picks = [found.astype(BF16), high.astype(BF16), low.astype(BF16)]
+        return picks, [block[:, LANES : LANES + wide_cols], cot, cot]
+
+    def spread(j):
+        picks, rows = choose(source(0, j), 0)
+        if not (isinstance(j, int) and j == half):
+            more_picks, more_rows = choose(source(1, j), 2 * CAP)
+            picks, rows = picks + more_picks, rows + more_rows
+        tsend[spread_rows(j), :] = lax.dot_general(
+            jnp.concatenate(picks, axis=0),
+            jnp.concatenate(rows, axis=0),
+            ROWS,
+            preferred_element_type=F32,
+        ).astype(BF16)
+
+        def start(k, carry):
+            spread_copy(j, k).start()
+            return carry
+
+        lax.fori_loop(1, peers, start, 0)
+        trecv[spread_rows(j, mine * GROUP, GROUP), :] = tsend[
+            spread_rows(j, mine * GROUP, GROUP), :
+        ]
+
+    def token_step(j):
+        for way in range(2):
+            token_arrival(way, j - 1).wait_recv()
+            if not (isinstance(j, int) and j == half):
+                token_send(way, j).start()
+        spread(j)
+
     pl.semaphore_wait(barrier, peers + 1)
+    for way in range(2):
+        token_send(way, 0).start()
 
     def group_rows(index):
         return pl.ds(pl.multiple_of(index * GROUP, GROUP), GROUP)
@@ -278,19 +422,38 @@
     pick_ref[2] = onehot(same & (spot == 0) & (upper == 1))
     pick_ref[3] = onehot(same & (spot == 1 + upper))
     gpart[...] = jnp.zeros_like(gpart)
+    row = iota((4 * few, wide), 0)
+    column = iota((4 * few, wide), 1)
+    slot = lax.rem(row, few)
+    spread_ref[...] = onehot(
+        (slot // CAP == column // GROUP)
+        & (lax.rem(column, GROUP) == (row // few) * CAP + lax.rem(slot, CAP))
+    )
 
     def rows_of(index, start=0, size=slots):
         return pl.ds(pl.multiple_of(index * slots + start, 16), size)
 
-    def source(way, j):
-        return lax.rem(me - j + steps, steps) if way == 0 else lax.rem(me + j, steps)
+    def spread_in(j):
+        spread_all(j).wait_recv()
+        both = not (isinstance(j, int) and j == half)
+        for at in range(peers // near):
+            found = jnp.dot(
+                spread_ref[...],
+                trecv[spread_rows(j, at * wide, wide), :],
+                preferred_element_type=F32,
+            ).astype(BF16)
+            for way in range(2 if both else 1):
+                here = rows_of(source(way, j), at * few, few)
+                base = 2 * way * few
+                xs[here, ring_cols:] = found[base : base + few, :]
+                cs[here, ring_cols:] = found[base + few : base + 2 * few, :]
 
     def gather(way, j, sub):
         buf = cs if sub else xs
         at = rows_of(source(way, j))
         return pltpu.make_async_remote_copy(
-            src_ref=buf.at[at],
-            dst_ref=buf.at[at],
+            src_ref=buf.at[at, pl.ds(0, ring_cols)],
+            dst_ref=buf.at[at, pl.ds(0, ring_cols)],
             send_sem=ag_send.at[way, j, sub],
             recv_sem=ag_recv.at[way, j, sub],
             device_id={"seq": left if way else right},
@@ -301,8 +464,8 @@
         buf = cs if sub else xs
         at = rows_of(source(way, j + 1))
         return pltpu.make_async_remote_copy(
-            src_ref=buf.at[at],
-            dst_ref=buf.at[at],
+            src_ref=buf.at[at, pl.ds(0, ring_cols)],
+            dst_ref=buf.at[at, pl.ds(0, ring_cols)],
             send_sem=ag_send.at[way, j, sub],
             recv_sem=ag_recv.at[way, j, sub],
             device_id={"seq": left if way else right},
@@ -356,6 +519,8 @@
         terms = terms + lax.dot_general(ones, low, COLS, preferred_element_type=F32)
         gpart[index, :, 0:slots] = terms
 
+    token_step(1)
+    token_step(2)
     exchange_wait(*forward)
     for sub, buf in enumerate((xs, cs)):
         for near_at in range(peers // near):
@@ -372,32 +537,40 @@
             buf[rows_of(me, near_at * few, few), :] = unstacked((one + two).astype(BF16), few)
         for way in range(2):
             gather(way, 0, sub).start()
-    loads[2].wait()
-    loads[3].wait()
+    loads[6].wait()
+    loads[7].wait()
     compute(me)
 
-    def ring_step(j, carry):
+    def pass_on(j):
         for sub in range(2):
             for way in range(2):
                 arrival(way, j - 1, sub).wait_recv()
                 gather(way, j, sub).start()
+
+    def ring_step(j, carry):
+        token_step(j + 2)
+        pass_on(j)
+        spread_in(j)
         compute(source(0, j))
         compute(source(1, j))
         return carry
 
-    lax.fori_loop(1, half - 1, ring_step, 0)
-
+    lax.fori_loop(1, half - 3, ring_step, 0)
     last = half - 1
+    ring_step(last - 2, 0)
+    ring_step(last - 1, 0)
     for sub in range(2):
         for way in range(2):
             arrival(way, last - 1, sub).wait_recv()
             if sub == way:
                 gather(way, last, sub).start()
-    compute(source(0, last))
-    compute(source(1, last))
-    scatter(0, 1, 1, direct=True).start()
-    scatter(1, 1, 0, direct=True).start()
+    spread_in(last)
+    for way in range(2):
+        compute(source(way, last))
+        for sub in fresh[1 - way]:
+            scatter(1 - way, 1, sub, direct=True).start()
     scatter_gate(1, 1, direct=True).start()
+    spread_in(half)
     arrival(0, last, 0).wait_recv()
     arrival(1, last, 1).wait_recv()
     compute(source(0, half))
@@ -417,25 +590,26 @@
         came = take[rows_of(at - 1, sub * SPLIT, SPLIT), :].astype(F32)
         give[rows_of(at, sub * SPLIT, SPLIT), :] = (ours + came).astype(BF16)
 
-    scatter(0, 0, 0, direct=True).start()
-    scatter(1, 0, 1, direct=True).start()
+    for way in range(2):
+        for sub in early[way]:
+            scatter(way, 0, sub, direct=True).start()
     scatter_gate(0, 0, direct=True).start()
     weights(0)
-    scatter(0, 0, 0, direct=True).wait_recv()
-    merge(0, 1, 0)
-    scatter(0, 1, 0).start()
-    scatter(1, 0, 1, direct=True).wait_recv()
-    merge(1, 1, 1)
-    scatter(1, 1, 1).start()
+    for at in range(len(early[0])):
+        for way in range(2):
+            sub = early[way][at]
+            scatter(way, 0, sub, direct=True).wait_recv()
+            merge(way, 1, sub)
+            scatter(way, 1, sub).start()
     scatter_gate(0, 0, direct=True).wait_recv()
     ggive[1] = gpart[target(0, 1)] + gtake[0]
     scatter_gate(0, 1).start()
     weights(1)
 
     def scatter_step(s, carry):
-        for order in range(2):
+        for at in range(count_sub):
             for way in range(2):
-                sub = (1 - order) if way == 0 else order
+                sub = (fresh[way] + early[way])[at]
                 scatter(way, s - 1, sub).wait_recv()
                 merge(way, s, sub)
                 scatter(way, s, sub).start()
@@ -450,12 +624,14 @@
     lax.fori_loop(2, half, scatter_step, 0)
 
     summed = []
-    for sub in range(2):
+    for sub in range(count_sub):
         whole = part[rows_of(me, sub * SPLIT, SPLIT), :].astype(F32)
         for way in range(2):
             scatter(way, last, sub).wait_recv()
             whole = whole + take[rows_of(way * half + last, sub * SPLIT, SPLIT), :].astype(F32)
         summed.append(whole.astype(BF16))
+    each = count_sub * near // peers
+    summed = [jnp.concatenate(summed[at : at + each], axis=0) for at in range(0, count_sub, each)]
     terms = gpart[me]
     for way in range(2):
         scatter_gate(way, last).wait_recv()
@@ -482,10 +658,14 @@
     exchange_end(*forward)
     for way in range(2):
         for s in range(half):
+            token_send(way, s).wait_send()
+            if way == 0:
+                spread_all(s + 1).wait_send()
             for sub in range(2):
                 if s < last or sub == way:
                     gather(way, s, sub).wait_send()
-                if s >= 1 or sub == way:
+            for sub in range(count_sub):
+                if s >= 1 or sub in early[way]:
                     scatter(way, s, sub).wait_send()
             if s >= 1 or way == 0:
                 scatter_gate(way, s).wait_send()
@@ -499,7 +679,7 @@
     column = iota((tokens_here, long), 1)
     scaled = []
     for k in range(2):
-        at = routes_ref[:, k : k + 1] * GROUP + 8 + spots[k]
+        at = routes[k] * GROUP + 8 + spots[k]
         found = jnp.dot(onehot(column == at), second, preferred_element_type=F32)
         scaled.append(found[:, 0:1] + found[:, LANES // 2 : LANES // 2 + 1])
     both = scaled[0] + scaled[1]
@@ -508,9 +688,7 @@
         one = (1.0 - sigmoids[k]) * (scaled[k] - gates[k] * both)
         logit_grad = logit_grad + jnp.where(chosen[k], one, 0.0)
     for piece in pieces(logit_grad, 3):
-        normed_grad = normed_grad + lax.dot_general(
-            piece, router, COLS, preferred_element_type=F32
-        )
+        normed_grad = normed_grad + jnp.dot(piece, router, preferred_element_type=F32)
     token = token_ref[...]
     inner_grad = normed_grad * gain_ref[...]
     slope = total(inner_grad * token) * (scale * scale * scale * (1.0 / width))
@@ -549,7 +727,7 @@
     long = peers * GROUP
     parts = width // LANES
     vmem = pl.BlockSpec(memory_space=pltpu.VMEM)
-    hbm = pl.BlockSpec(memory_space=pl.ANY)
+    hbm = pl.BlockSpec(memory_space=pltpu.HBM)
     dma = pltpu.SemaphoreType.DMA
     gemb, gin, gout = pl.pallas_call(
         functools.partial(block_step, steps, peers),
@@ -558,13 +736,17 @@
             jax.ShapeDtypeStruct((width, hidden), F32),
             jax.ShapeDtypeStruct((hidden, width), F32),
         ),
-        in_specs=[hbm, vmem, vmem, vmem, vmem, hbm, hbm, hbm],
+        in_specs=[hbm] * 8,
         out_specs=(vmem,) * 3,
         scratch_shapes=[
             pltpu.VMEM((count, width), BF16),
             pltpu.VMEM((tokens_here, width), BF16),
             pltpu.VMEM((width, hidden), BF16),
             pltpu.VMEM((hidden, width), BF16),
+            pltpu.VMEM((1, width), F32),
+            pltpu.VMEM((1, width), F32),
+            pltpu.VMEM((peers, width), BF16),
+            pltpu.VMEM((2, tokens_here), jnp.int32),
             pltpu.VMEM((count, width), F32),
             pltpu.VMEM((tokens_here, width), F32),
             pltpu.VMEM((long, 3 * LANES), BF16),
@@ -573,6 +755,10 @@
             pltpu.VMEM((long, 2 * LANES), BF16),
             pltpu.VMEM((2, parts * tokens_here, long), BF16),
             pltpu.VMEM((4, parts * 16 * CAP, 16 * GROUP), BF16),
+            pltpu.VMEM((4 * 16 * CAP, 16 * GROUP), BF16),
+            pltpu.VMEM((steps * tokens_here, (1 + 2 * SPREAD) * LANES), BF16),
+            pltpu.VMEM((half * long, SPREAD * LANES), BF16),
+            pltpu.VMEM((half * long, SPREAD * LANES), BF16),
             pltpu.VMEM((steps * slots, width), BF16),
             pltpu.VMEM((steps * slots, width), BF16),
             pltpu.VMEM((steps * slots, hidden), BF16),
@@ -583,15 +769,19 @@
             pltpu.VMEM((steps * slots, width), BF16),
             pltpu.VMEM((steps, 8, LANES), F32),
             pltpu.VMEM((steps, 8, LANES), F32),
-            dma((4,)),
+            dma((8,)),
             dma((peers,)),
             dma((peers,)),
             dma((peers,)),
             dma((peers,)),
+            dma((2, half)),
+            dma((2, half)),
+            dma((half,)),
+            dma((half,)),
             dma((2, half, 2)),
             dma((2, half, 2)),
-            dma((2, half, 2)),
-            dma((2, half, 2)),
+            dma((2, half, slots // SPLIT)),
+            dma((2, half, slots // SPLIT)),
             dma((2, half)),
             dma((2, half)),
         ],
@@ -602,8 +792,8 @@
         byte_embed[0],
         score_weight[None],
         norm_gain[None],
-        router,
-        routes[0],
+        router.T,
+        routes[0].T,
         expert_in[0],
         expert_out[0],
         cotangent[0],

time: 148 us -> 133 us (0.90)
  Pallas kernels: 139 us -> 122 us
    pallas_call x1, Pallas kernels: 139 us -> 122 us  [per_device(): pl.pallas_call(functools.partial(block_step, steps, peers), out_shape=(ja...]
    unnamed x18 -> x21, local copies, waits for them, and re-layouts: 7.16 us -> 9.43 us
where the time goes in v3:
time: 133 us; the launch traced here: 132 us
  Pallas kernels  122 us (92%)
  local copies, waits for them, and re-layouts  9.43 us (7%)
    pallas_call x1, Pallas kernels, per_device(): pl.pallas_call(functools.partial(block_step, steps, peers), out_shape=(ja...  122 us
    unnamed x21, local copies, waits for them, and re-layouts  9.43 us

profile of v3, /device:TPU:1, one launch (start us, length us, event | category | flops | bytes accessed | tf_op | source)
XLA Modules:
  0.0 132.2 jit_solution(6254512332636721943)
XLA Ops:
  0.6 0.0 copy-start.6
  0.6 0.0 copy-start.5
  0.7 0.0 copy-start.7
  0.7 0.7 copy-done.6
  1.3 0.0 copy-done.5
  1.3 0.0 copy-done.7
  1.3 0.0 copy-start
  1.3 1.0 copy-done
  2.4 0.0 copy-start.1
  2.4 1.0 copy-done.1
  3.4 0.0 copy-start.2
  3.4 0.9 copy-done.2
  4.4 0.0 copy-start.3
  4.4 0.8 copy-done.3
  5.2 0.0 copy-start.4
  5.2 0.8 copy-done.4
  6.1 122.1 %shard_map.103 = (bf16[128,1024]{1,0:T(8,128)(2,1)S(1)}, f32[1024,256]{1,0:T(8,128)}, f32[256,1024]{1,0:T(8,128)}) custom-call(bf16[128,1024]{1,0:T(8,128)(2,1)S(1)} %bitcast.15, f32[1,1024]{1,0:T(1,128)S(1)} %bitcast.19, f32[1,1024]{1,0:T(1,128)S(1)} %bitcast.20, bf16[32,1024]{1,0:T(8,128)(2,1)S(1)} %bitcast.17, s32[2,32]{1,0:T(2,128)S(1)} %bitcast.21, ...), custom_call_target="tpu_custom_call" | custom-call | tf_op jit(solution)/shard_map/pallas_call | solution.py:732
  128.1 0.7 copy.14
  128.8 0.0 copy-start.8
  128.8 2.4 %copy.15 = f32[1,1024,256]{2,1,0:T(8,128)} copy(f32[1,1024,256]{2,1,0:T(8,128)} %bitcast.23) | data formatting | bytes 2097152
  131.2 0.0 copy-done.8
  131.2 1.0 copy.16
Async XLA Ops:
  0.6 0.7 copy-start.6
  0.6 0.7 copy-start.5
  0.7 0.7 copy-start.7
  1.3 1.0 copy-start
  2.4 1.0 copy-start.1
  3.4 0.9 copy-start.2
  4.4 0.8 copy-start.3
  5.2 0.8 copy-start.4
  128.8 2.4 %copy-start.8 = (f32[256,1024]{1,0:T(8,128)S(1)}, f32[256,1024]{1,0:T(8,128)}, u32[]{:S(2)}) copy-start(f32[256,1024]{1,0:T(8,128)} %get-tuple-element.8) | copy-start | bytes 3145732

commit v4 on v3

--- a/solution.py
+++ b/solution.py
@@ -11,8 +11,8 @@
 INV_ROOT_TWO_PI = 0.3989422804014327
 MESH = pl.DeviceIdType.MESH
 LANES = 128
-SPLIT = 48
-SPREAD = 3
+SPLIT = 16
+SPREAD = 4
 CAP = 3
 GROUP = 16
 ROWS = (((0,), (0,)), ((), ()))
@@ -786,7 +786,7 @@
             dma((2, half)),
         ],
         compiler_params=pltpu.CompilerParams(
-            collective_id=0, has_side_effects=True, vmem_limit_bytes=52 * 1024 * 1024
+            collective_id=0, has_side_effects=True, vmem_limit_bytes=67043328
         ),
     )(
         byte_embed[0],

time: 133 us -> 121 us (0.910)
  Pallas kernels: 122 us -> 115 us
  local copies, waits for them, and re-layouts: 9.43 us -> 4.99 us
    pallas_call x1, Pallas kernels: 122 us -> 115 us  [per_device(): pl.pallas_call(functools.partial(block_step, steps, peers), out_shape=(ja...]
    unnamed x21 -> x5, local copies, waits for them, and re-layouts: 9.43 us -> 4.99 us
where the time goes in v4:
time: 121 us
  Pallas kernels  115 us (95%)
  local copies, waits for them, and re-layouts  4.99 us (4%)
    pallas_call x1, Pallas kernels, per_device(): pl.pallas_call(functools.partial(block_step, steps, peers), out_shape=(ja...  115 us
    unnamed x5, local copies, waits for them, and re-layouts  4.99 us

profile of v4, /device:TPU:1, one launch (start us, length us, event | category | flops | bytes accessed | tf_op | source)
XLA Modules:
  0.0 121.0 jit_solution(7754899276945944484)
XLA Ops:
  0.6 115.3 %shard_map.103 = (bf16[128,1024]{1,0:T(8,128)(2,1)}, f32[1024,256]{1,0:T(8,128)}, f32[256,1024]{1,0:T(8,128)}) custom-call(bf16[128,1024]{1,0:T(8,128)(2,1)} %bitcast.17, f32[1,1024]{1,0:T(1,128)} %bitcast.21, f32[1,1024]{1,0:T(1,128)} %bitcast.22, bf16[32,1024]{1,0:T(8,128)(2,1)} %bitcast.19, s32[2,32]{1,0:T(2,128)} %bitcast.23, ...), custom_call_target="tpu_custom_call" | custom-call | tf_op jit(solution)/shard_map/pallas_call | solution.py:732
  116.0 1.7 %copy.14 = bf16[1,128,1024]{2,1,0:T(8,128)(2,1)} copy(bf16[1,128,1024]{2,1,0:T(8,128)(2,1)} %bitcast.18) | data formatting | bytes 524288
  117.6 0.0 copy-start
  117.6 2.4 %copy.15 = f32[1,1024,256]{2,1,0:T(8,128)} copy(f32[1,1024,256]{2,1,0:T(8,128)} %bitcast.14) | data formatting | bytes 2097152
  120.0 0.0 copy-done
  120.0 1.0 copy.16
Async XLA Ops:
  117.6 2.4 %copy-start = (f32[256,1024]{1,0:T(8,128)S(1)}, f32[256,1024]{1,0:T(8,128)}, u32[]{:S(2)}) copy-start(f32[256,1024]{1,0:T(8,128)} %get-tuple-element.8) | copy-start | bytes 3145732

commit v5 on v4

--- a/solution.py
+++ b/solution.py
@@ -64,6 +64,8 @@
     wout_hbm,
     cot_hbm,
     gemb_ref,
+    gin_hbm,
+    gout_hbm,
     gin_ref,
     gout_ref,
     emb_ref,
@@ -622,6 +624,12 @@
         return carry
 
     lax.fori_loop(2, half, scatter_step, 0)
+    stores = [
+        pltpu.make_async_copy(src, dst, in_sem.at[at])
+        for at, (src, dst) in enumerate(((gin_ref, gin_hbm), (gout_ref, gout_hbm)))
+    ]
+    for store in stores:
+        store.start()
 
     summed = []
     for sub in range(count_sub):
@@ -713,6 +721,45 @@
         shuffle, jnp.concatenate(result, axis=0), preferred_element_type=F32
     ).astype(BF16)
     exchange_end(*backward)
+    for store in stores:
+        store.wait()
+
+
+def hand_on(count, *refs):
+    sources, results, buffers = refs[:count], refs[count : 2 * count], refs[2 * count : -2]
+    load_sem, store_sem = refs[-2:]
+    loads, stores = [], []
+    for source, result, buffer in zip(sources, results, buffers):
+        rows = min(source.shape[0], 128)
+        for start in range(0, source.shape[0], rows):
+            span, at = pl.ds(start, rows), len(loads)
+            loads.append(
+                pltpu.make_async_copy(source.at[span], buffer.at[span], load_sem.at[at])
+            )
+            stores.append(
+                pltpu.make_async_copy(buffer.at[span], result.at[span], store_sem.at[at])
+            )
+    for load in loads:
+        load.start()
+    for load, store in zip(loads, stores):
+        load.wait()
+        store.start()
+    for store in stores:
+        store.wait()
+
+
+def handed_on(*arrays):
+    hbm = pl.BlockSpec(memory_space=pltpu.HBM)
+    pieces_all = sum(-(-a.shape[0] // 128) for a in arrays)
+    return pl.pallas_call(
+        functools.partial(hand_on, len(arrays)),
+        out_shape=tuple(jax.ShapeDtypeStruct(a.shape, a.dtype) for a in arrays),
+        in_specs=[hbm] * len(arrays),
+        out_specs=(hbm,) * len(arrays),
+        scratch_shapes=[pltpu.VMEM(a.shape, a.dtype) for a in arrays]
+        + [pltpu.SemaphoreType.DMA((pieces_all,))] * 2,
+        compiler_params=pltpu.CompilerParams(vmem_limit_bytes=67043328),
+    )(*arrays)
 
 
 def per_device(
@@ -737,8 +784,10 @@
             jax.ShapeDtypeStruct((hidden, width), F32),
         ),
         in_specs=[hbm] * 8,
-        out_specs=(vmem,) * 3,
+        out_specs=(vmem, hbm, hbm),
         scratch_shapes=[
+            pltpu.VMEM((width, hidden), F32),
+            pltpu.VMEM((hidden, width), F32),
             pltpu.VMEM((count, width), BF16),
             pltpu.VMEM((tokens_here, width), BF16),
             pltpu.VMEM((width, hidden), BF16),
@@ -798,6 +847,7 @@
         expert_out[0],
         cotangent[0],
     )
+    gin, gout, gemb = handed_on(gin, gout, gemb)
     return (gemb[None], gin[None], gout[None])
 
 

time: 121 us -> 118 us (0.975)
  local copies, waits for them, and re-layouts: 4.99 us -> 0 us
  Pallas kernels: 115 us -> 117 us
    unnamed x5 -> x0, local copies, waits for them, and re-layouts: 4.99 us -> none
    pallas_call x0 -> x1, Pallas kernels: none -> 2.7 us  [handed_on(): pl.pallas_call(functools.partial(hand_on, len(arrays)), out_shape=tuple((...]
where the time goes in v5:
time: 118 us
  Pallas kernels  117 us (99%)
    pallas_call x1, Pallas kernels, per_device(): pl.pallas_call(functools.partial(block_step, steps, peers), out_shape=(ja...  115 us
    pallas_call x1, Pallas kernels, handed_on(): pl.pallas_call(functools.partial(hand_on, len(arrays)), out_shape=tuple((...  2.7 us

profile of v5, /device:TPU:1, one launch (start us, length us, event | category | flops | bytes accessed | tf_op | source)
XLA Modules:
  0.0 117.9 jit_solution(9817157950291157407)
XLA Ops:
  0.6 114.6 %shard_map.103 = (bf16[128,1024]{1,0:T(8,128)(2,1)}, f32[1024,256]{1,0:T(8,128)}, f32[256,1024]{1,0:T(8,128)}) custom-call(bf16[128,1024]{1,0:T(8,128)(2,1)} %bitcast.15, f32[1,1024]{1,0:T(1,128)} %bitcast.18, f32[1,1024]{1,0:T(1,128)} %bitcast.19, bf16[32,1024]{1,0:T(8,128)(2,1)} %bitcast.16, s32[2,32]{1,0:T(2,128)} %bitcast.20, ...), custom_call_target="tpu_custom_call" | custom-call | tf_op jit(solution)/shard_map/pallas_call | solution.py:779
  115.2 2.7 %shard_map.104 = (f32[1024,256]{1,0:T(8,128)}, f32[256,1024]{1,0:T(8,128)}, bf16[128,1024]{1,0:T(8,128)(2,1)}) custom-call(f32[1024,256]{1,0:T(8,128)} %get-tuple-element.9.refs_0_, f32[256,1024]{1,0:T(8,128)} %get-tuple-element.10.refs_1_, bf16[128,1024]{1,0:T(8,128)(2,1)} %get-tuple-element.11.refs_2_), custom_call_target="tpu_custom_call" | custom-call | tf_op jit(solution)/shard_map/pallas_call | solution.py:754
